TPU v7x, 512 devices: a whole 4x8x8 slice. The times are simulated.
512 devices in a mesh: seq: 64 (over y_hi, z, core), tp: 8 (over x, y_lo).
Axes of the slice: x: 4, y: 8 (y_hi: 4, y_lo: 2; y = y_hi * 2 + y_lo), z: 8, core: 2. Of those that a mesh axis runs over, the one named last changes fastest.
Arguments:
- frames_in: bfloat16 [1536, 32768], P('tp', 'seq'), may hold values from -30 to 30
- norm_gain: float32 [1536], P('tp'), may hold values from 0.5 to 2
- value_weight: bfloat16 [1536, 1536], P('tp'), may hold values from -0.15625 to 0.15625
- gate_weight: bfloat16 [1536, 1536], P('tp'), may hold values from -0.15625 to 0.15625
- depth_kernel: float32 [1536, 32], P('tp'), may hold values from -6 to 6
- conv_gain: float32 [1536], P('tp'), may hold values from 0.5 to 2
- out_weight: bfloat16 [1536, 1536], P('tp'), may hold values from -0.15625 to 0.15625
- cotangent: bfloat16 [1536, 32768], P('tp', 'seq'), may hold values from -15 to 15
Outputs:
- block_out: bfloat16 [1536, 32768], P('tp', 'seq')
- input_grad: bfloat16 [1536, 32768], P('tp', 'seq')
- grad_norm_gain: float32 [1536], P('tp')
- grad_value: bfloat16 [1536, 1536], P('tp')
- grad_gate: bfloat16 [1536, 1536], P('tp')
- grad_kernel: float32 [1536, 32], P('tp')
- grad_conv_gain: float32 [1536], P('tp')
- grad_out: bfloat16 [1536, 1536], P('tp')
All inputs are finite; a program needn't handle non-finite values.
Results may differ from a plain program's by a relative error of at most 0.027.
Values may be sent and summed in bfloat16 or wider, within the bound.
A program may use at most 64 MiB of HBM per device.

v0:
```python
import jax
import jax.numpy as jnp
from jax import lax
from jax.sharding import PartitionSpec as P

EPS = 1e-05


def with_halo(cells, sides, width):
    for axis, dim in sides:
        count = lax.axis_size(axis)
        ends = count - 1
        head = lax.slice_in_dim(cells, 0, width, axis=dim)
        tail = lax.slice_in_dim(cells, cells.shape[dim] - width, cells.shape[dim], axis=dim)
        cells = jnp.concatenate(
            [
                lax.ppermute(tail, axis, [(i, (i + 1) % count) for i in range(ends)]),
                cells,
                lax.ppermute(head, axis, [((i + 1) % count, i) for i in range(ends)]),
            ],
            axis=dim,
        )
    return cells


def widen(values):
    return lax.optimization_barrier(values).astype(jnp.float32)


def row_sums(values):
    return lax.psum(values, "tp")


def split_norm(values, width):
    mean = row_sums(jnp.sum(values, axis=0, keepdims=True)) / width
    centred = values - mean
    spread = row_sums(jnp.sum(centred * centred, axis=0, keepdims=True)) / width
    inverse = lax.rsqrt(spread + EPS)
    return (centred * inverse, inverse)


def split_norm_back(d_hat, hat, inverse, width):
    first, second = row_sums(
        (jnp.sum(d_hat, axis=0, keepdims=True), jnp.sum(d_hat * hat, axis=0, keepdims=True))
    )
    return (d_hat - first / width - hat * (second / width)) * inverse


def spread_channels(values):
    return lax.all_gather(values, "tp", axis=0, tiled=True)


def frame_rims(values, reach):
    return with_halo(values, (("seq", 1),), reach)


def reduce_inputs(term):
    rounded = widen(term.astype(jnp.bfloat16))
    return lax.psum_scatter(
        rounded.astype(jnp.bfloat16), "tp", scatter_dimension=0, tiled=True
    ).astype(jnp.float32)


def contract_rows(left, right):
    return lax.dot_general(
        left, right, (((0,), (0,)), ((), ())), preferred_element_type=jnp.float32
    )


def contract_cols(left, right):
    return lax.dot_general(
        left, right, (((1,), (1,)), ((), ())), preferred_element_type=jnp.float32
    )


def local(
    frames_in, norm_gain, value_weight, gate_weight, depth_kernel, conv_gain, out_weight, cotangent
):
    chans, row_count = frames_in.shape
    parts = lax.axis_size("tp")
    width = chans * parts
    taps = depth_kernel.shape[1]
    reach = taps // 2
    scale = float(row_count * lax.axis_size("seq")) ** (-0.5)
    inputs = frames_in.astype(jnp.float32)
    hat_in, inverse_in = split_norm(inputs, width)
    normed = (hat_in * norm_gain[:, None]).astype(jnp.bfloat16)
    normed_all = spread_channels(normed)
    value = jnp.dot(value_weight, normed_all, preferred_element_type=jnp.float32)
    gate = jnp.dot(gate_weight, normed_all, preferred_element_type=jnp.float32)
    gate_sig = jax.nn.sigmoid(gate)
    glu = (value * gate_sig).astype(jnp.bfloat16)
    glu_wide = widen(frame_rims(glu, reach))
    conv = jnp.zeros((chans, row_count), jnp.float32)
    for tap in range(taps):
        conv = conv + depth_kernel[:, tap : tap + 1] * glu_wide[:, tap : tap + row_count]
    hat_conv, inverse_conv = split_norm(conv, width)
    scaled = hat_conv * conv_gain[:, None]
    swish_sig = jax.nn.sigmoid(scaled)
    act = (scaled * swish_sig).astype(jnp.bfloat16)
    act_all = spread_channels(act)
    block_out = (inputs + jnp.dot(out_weight, act_all, preferred_element_type=jnp.float32)).astype(
        jnp.bfloat16
    )
    grad_out = contract_cols(cotangent, act_all) * scale
    d_act = reduce_inputs(contract_rows(out_weight, cotangent))
    d_scaled = d_act * (swish_sig + scaled * swish_sig * (1.0 - swish_sig))
    grad_conv_gain = jnp.sum(d_scaled * hat_conv, axis=1) * scale
    d_conv = split_norm_back(d_scaled * conv_gain[:, None], hat_conv, inverse_conv, width).astype(
        jnp.bfloat16
    )
    d_conv_f = widen(d_conv)
    d_conv_wide = widen(frame_rims(d_conv, reach))
    d_glu = jnp.zeros((chans, row_count), jnp.float32)
    kernel_cols = []
    for tap in range(taps):
        start = 2 * reach - tap
        d_glu = d_glu + depth_kernel[:, tap : tap + 1] * d_conv_wide[:, start : start + row_count]
        kernel_cols.append(jnp.sum(glu_wide[:, tap : tap + row_count] * d_conv_f, axis=1))
    grad_kernel = jnp.stack(kernel_cols, axis=1) * scale
    d_value = (d_glu * gate_sig).astype(jnp.bfloat16)
    d_gate = (d_glu * value * gate_sig * (1.0 - gate_sig)).astype(jnp.bfloat16)
    grad_value = contract_cols(d_value, normed_all) * scale
    grad_gate = contract_cols(d_gate, normed_all) * scale
    d_normed = reduce_inputs(
        contract_rows(value_weight, d_value) + contract_rows(gate_weight, d_gate)
    )
    grad_norm_gain = jnp.sum(d_normed * hat_in, axis=1) * scale
    input_grad = (
        cotangent.astype(jnp.float32)
        + split_norm_back(d_normed * norm_gain[:, None], hat_in, inverse_in, width)
    ).astype(jnp.bfloat16)
    grad_out, grad_kernel, grad_conv_gain, grad_value, grad_gate, grad_norm_gain = lax.psum(
        (grad_out, grad_kernel, grad_conv_gain, grad_value, grad_gate, grad_norm_gain), "seq"
    )
    return (
        block_out,
        input_grad,
        grad_norm_gain,
        grad_value.astype(jnp.bfloat16),
        grad_gate.astype(jnp.bfloat16),
        grad_kernel,
        grad_conv_gain,
        grad_out.astype(jnp.bfloat16),
    )


def solution(mesh):
    return jax.shard_map(
        local,
        mesh=mesh,
        in_specs=(
            P("tp", "seq"),
            P("tp"),
            P("tp", None),
            P("tp", None),
            P("tp", None),
            P("tp"),
            P("tp", None),
            P("tp", "seq"),
        ),
        out_specs=(
            P("tp", "seq"),
            P("tp", "seq"),
            P("tp"),
            P("tp", None),
            P("tp", None),
            P("tp", None),
            P("tp"),
            P("tp", None),
        ),
        check_vma=False,
    )
```

profile of v0, /device:TPU:1, one launch (start us, length us, event | category | flops | bytes accessed | tf_op | source)
XLA Modules:
  0.0 617.3 jit_solution(990302388884489150)
XLA Ops:
  7.2 0.0 copy-start
  7.2 0.0 all-gather.3.cloned.1.call-start
  7.2 1.0 convert_reduce_fusion
  8.3 16.9 %psum.98 = f32[1,512]{1,0:T(1,128)S(1)} all-reduce(f32[1,512]{1,0:T(1,128)S(1)} %bitcast.194), channel_id=1, replica_groups=mesh['seq'=64,'tp'=8] {'tp'}, use_global_device_ids=true, to_apply=%region_1.0 | all-reduce | flops 512 | bytes 4096 | tf_op jit(solution)/shard_map/psum | solution.py:31
  25.1 1.0 fusion.21
  26.1 12.7 %psum.99 = f32[1,512]{1,0:T(1,128)S(1)} all-reduce(f32[1,512]{1,0:T(1,128)S(1)} %bitcast.195), channel_id=1, replica_groups=mesh['seq'=64,'tp'=8] {'tp'}, use_global_device_ids=true, to_apply=%region_3.0 | all-reduce | flops 512 | bytes 4096 | tf_op jit(solution)/shard_map/psum | solution.py:31
  38.8 1.7 fusion.16
  40.6 0.0 all-gather.3.cloned.1.call-update
  40.6 0.0 copy-start.11
  40.6 0.0 reduce-scatter.3.cloned.1.call-start
  40.7 2.9 convolution_convert_fusion
  43.6 0.0 reduce-scatter.3.cloned.1.call-update
  43.6 0.0 all-gather.5.cloned.1.call-start
  43.7 52.5 %all-gather.3.cloned.1.call-done = bf16[1536,512]{1,0:T(8,128)(2,1)} async-done(((bf16[192,512]{1,0:T(8,128)(2,1)}), bf16[1536,512]{1,0:T(8,128)(2,1)}) %all-gather.3.cloned.1.call-update) | async-done | bytes 1572880 | tf_op jit(solution)/shard_map/all_gather | solution.py:50
  96.2 2.1 fusion.6
  98.3 1.2 multiply_convert_fusion.3
  99.5 0.1 fusion.91
  99.6 6.1 collective-permute-start
  105.7 1.9 collective-permute-start.1
  107.8 0.0 copy-start.21
  107.8 0.0 copy-start.22
  107.8 3.4 collective-permute-done.1
  111.2 0.1 pad_maximum_fusion
  111.4 4.6 fusion.89
  116.1 16.0 %psum.100 = f32[1,512]{1,0:T(1,128)S(1)} all-reduce(f32[1,512]{1,0:T(1,128)S(1)} %bitcast.199), channel_id=1, replica_groups=mesh['seq'=64,'tp'=8] {'tp'}, use_global_device_ids=true, to_apply=%region_5.0 | all-reduce | flops 512 | bytes 4096 | tf_op jit(solution)/shard_map/psum | solution.py:31
  132.1 0.1 multiply_reduce_fusion.2
  132.2 14.8 %psum.101 = f32[1,512]{1,0:T(1,128)S(1)} all-reduce(f32[1,512]{1,0:T(1,128)S(1)} %bitcast.196), channel_id=1, replica_groups=mesh['seq'=64,'tp'=8] {'tp'}, use_global_device_ids=true, to_apply=%region_7.0 | all-reduce | flops 512 | bytes 4096 | tf_op jit(solution)/shard_map/psum | solution.py:31
  147.0 0.5 reduce-scatter.3.cloned.1.call-done
  147.4 2.6 multiply_reduce_fusion
  150.0 14.8 %all-reduce.2 = (f32[1,512]{1,0:T(1,128)S(1)}, f32[1,512]{1,0:T(1,128)S(1)}) all-reduce(f32[1,512]{1,0:T(1,128)S(1)} %bitcast.190, f32[1,512]{1,0:T(1,128)S(1)} %bitcast.191), channel_id=1, replica_groups=mesh['seq'=64,'tp'=8] {'tp'}, use_global_device_ids=true, to_apply=%region_12.0 | all-reduce | flops 1024 | bytes 8192 | tf_op jit(solution)/shard_map/psum | solution.py:31
  164.8 1.9 multiply_convert_fusion.2
  166.7 0.0 all-gather.5.cloned.1.call-update
  166.7 0.0 reduce-scatter.5.cloned.1.call-start
  166.8 0.1 fusion.90
  166.9 10.1 %collective-permute-start.2 = (bf16[192,16]{1,0:T(8,128)(2,1)S(1)}, bf16[192,16]{1,0:T(8,128)(2,1)S(1)}, u32[]{:S(2)}, u32[]{:S(2)}) collective-permute-start(bf16[192,16]{1,0:T(8,128)(2,1)S(1)} %get-tuple-element.63), channel_id=1, source_target_pairs={{0,8},{8,16},{16,24},{24,32},{32,40},{40,48},{48,56},{56,64},{64,7... | collective-permute-start | bytes 18440 | tf_op jit(solution)/shard_map/ppermute | solution.py:17
  176.9 2.1 collective-permute-start.3
  179.1 3.3 collective-permute-done.3
  182.3 0.1 pad_maximum_fusion.1
  182.5 0.0 copy-start.6
  182.6 5.8 multiply_convert_fusion
  188.4 0.1 multiply_convert_fusion.1
  188.5 0.7 fusion.94
  189.2 0.5 copy-done.12
  189.6 1.8 fusion.1
  191.4 0.0 reduce-scatter.5.cloned.1.call-update
  191.4 2.1 fusion.54
  193.5 2.8 fusion.55
  196.3 0.1 stack.131
  196.4 0.6 broadcast_multiply_fusion.7
  197.0 0.6 broadcast_multiply_fusion
  197.6 0.7 convolution_multiply_fusion.1
  198.3 0.0 copy-start.8
  198.3 2.7 convolution_multiply_fusion.2
  200.9 16.9 %all-gather.5.cloned.1.call-done = bf16[1536,512]{1,0:T(8,128)(2,1)} async-done(((bf16[192,512]{1,0:T(8,128)(2,1)}), bf16[1536,512]{1,0:T(8,128)(2,1)}) %all-gather.5.cloned.1.call-update) | async-done | bytes 1572880 | tf_op jit(solution)/shard_map/all_gather | solution.py:50
  217.8 3.2 fusion.2
  221.1 0.0 copy-start.14
  221.1 1.2 fusion.8
  222.3 45.8 %reduce-scatter.5.cloned.1.call-done = bf16[192,512]{1,0:T(8,128)(2,1)} async-done(((bf16[1536,512]{1,0:T(8,128)(2,1)}), bf16[192,512]{1,0:T(8,128)(2,1)}) %reduce-scatter.5.cloned.1.call-update) | async-done | bytes 196624 | tf_op jit(solution)/shard_map/reduce_scatter | solution.py:59
  268.1 1.1 fusion.23
  269.2 0.6 broadcast_multiply_fusion.8
  269.8 14.8 %all-reduce.1 = (f32[1,512]{1,0:T(1,128)S(1)}, f32[1,512]{1,0:T(1,128)S(1)}) all-reduce(f32[1,512]{1,0:T(1,128)S(1)} %bitcast.192, f32[1,512]{1,0:T(1,128)S(1)} %bitcast.193), channel_id=1, replica_groups=mesh['seq'=64,'tp'=8] {'tp'}, use_global_device_ids=true, to_apply=%region_17.0 | all-reduce | flops 1024 | bytes 8192 | tf_op jit(solution)/shard_map/psum | solution.py:31
  284.6 0.6 broadcast_multiply_fusion.2
  285.2 324.0 %all-reduce.4 = (f32[192]{0:T(256)}, bf16[192,1536]{1,0:T(8,128)(2,1)}, bf16[192,1536]{1,0:T(8,128)(2,1)}, f32[192,32]{0,1:T(8,128)}, f32[192]{0:T(256)}, /*index=5*/bf16[192,1536]{1,0:T(8,128)(2,1)}) all-reduce(f32[192]{0:T(256)} %broadcast_multiply_fusion.8, ...), channel_id=1, replica_groups=mesh['seq'=64,'tp'=8] {'seq'}, use_global_device_ids=true, to_apply=%region_19.0 | all-reduce | flops 891264 | bytes 5360640 | tf_op jit(solution)/shard_map/psum | solution.py:133
  609.2 1.5 fusion.20
  (54 shorter events, 0.3 us)
Async XLA Ops:
  7.2 91.1 %copy-start = (bf16[192,1536]{1,0:T(8,128)(2,1)S(1)}, bf16[192,1536]{1,0:T(8,128)(2,1)}, u32[]{:S(2)}) copy-start(bf16[192,1536]{1,0:T(8,128)(2,1)} %param.10) | copy-start | bytes 1769476
  7.2 89.0 %all-gather.3.cloned.1.call-start = ((), (), s32[]{:S(2)}) async-start(), calls=%async_computation.2 | async-start | bytes 1769472 | tf_op jit(solution)/shard_map/all_gather | solution.py:50
  40.6 3.1 copy-start.13
  40.6 55.6 %copy-start.11 = (bf16[192,1536]{1,0:T(8,128)(2,1)S(1)}, bf16[192,1536]{1,0:T(8,128)(2,1)}, u32[]{:S(2)}) copy-start(bf16[192,1536]{1,0:T(8,128)(2,1)} %param.11) | copy-start | bytes 1769476
  40.6 106.8 %reduce-scatter.3.cloned.1.call-start = ((), (), s32[]{:S(2)}) async-start(), calls=%async_computation.4 | async-start | bytes 1769472 | tf_op jit(solution)/shard_map/reduce_scatter | solution.py:59
  43.6 174.2 %all-gather.5.cloned.1.call-start = ((), (), s32[]{:S(2)}) async-start(), calls=%async_computation.3 | async-start | bytes 1769472 | tf_op jit(solution)/shard_map/all_gather | solution.py:50
  96.2 2.1 copy-start.1
  98.3 1.2 copy-start.5
  99.6 8.2 %collective-permute-start = (bf16[192,16]{1,0:T(8,128)(2,1)S(1)}, bf16[192,16]{1,0:T(8,128)(2,1)S(1)}, u32[]{:S(2)}, u32[]{:S(2)}) collective-permute-start(bf16[192,16]{1,0:T(8,128)(2,1)S(1)} %get-tuple-element.65), channel_id=1, source_target_pairs={{0,8},{8,16},{16,24},{24,32},{32,40},{40,48},{48,56},{56,64},{64,7... | collective-permute-start | bytes 18440 | tf_op jit(solution)/shard_map/ppermute | solution.py:17
  105.7 5.4 collective-permute-start.1
  107.7 8.3 %copy-start.15 = (f32[192,1]{0,1:T(1,128)}, f32[192,1]{0,1:T(1,128)S(1)}, u32[]{:S(2)}) copy-start(f32[192,1]{0,1:T(1,128)S(1)} %get-tuple-element.91) | copy-start | bytes 2308
  107.7 8.3 %copy-start.16 = (f32[192,1]{0,1:T(1,128)}, f32[192,1]{0,1:T(1,128)S(1)}, u32[]{:S(2)}) copy-start(f32[192,1]{0,1:T(1,128)S(1)} %get-tuple-element.92) | copy-start | bytes 2308
  107.7 8.3 %copy-start.17 = (f32[192,1]{0,1:T(1,128)}, f32[192,1]{0,1:T(1,128)S(1)}, u32[]{:S(2)}) copy-start(f32[192,1]{0,1:T(1,128)S(1)} %get-tuple-element.93) | copy-start | bytes 2308
  107.7 8.3 %copy-start.18 = (f32[192,1]{0,1:T(1,128)}, f32[192,1]{0,1:T(1,128)S(1)}, u32[]{:S(2)}) copy-start(f32[192,1]{0,1:T(1,128)S(1)} %get-tuple-element.94) | copy-start | bytes 2308
  107.7 8.3 %copy-start.19 = (f32[192,1]{0,1:T(1,128)}, f32[192,1]{0,1:T(1,128)S(1)}, u32[]{:S(2)}) copy-start(f32[192,1]{0,1:T(1,128)S(1)} %get-tuple-element.95) | copy-start | bytes 2308
  107.8 8.3 %copy-start.20 = (f32[192,1]{0,1:T(1,128)}, f32[192,1]{0,1:T(1,128)S(1)}, u32[]{:S(2)}) copy-start(f32[192,1]{0,1:T(1,128)S(1)} %get-tuple-element.96) | copy-start | bytes 2308
  107.8 8.3 %copy-start.21 = (f32[192,1]{0,1:T(1,128)}, f32[192,1]{0,1:T(1,128)S(1)}, u32[]{:S(2)}) copy-start(f32[192,1]{0,1:T(1,128)S(1)} %get-tuple-element.97) | copy-start | bytes 2308
  107.8 8.3 %copy-start.22 = (f32[192,1]{0,1:T(1,128)}, f32[192,1]{0,1:T(1,128)S(1)}, u32[]{:S(2)}) copy-start(f32[192,1]{0,1:T(1,128)S(1)} %get-tuple-element.98) | copy-start | bytes 2308
  111.4 36.1 %copy-start.24 = (f32[192]{0:T(256)S(1)}, f32[192]{0:T(256)}, u32[]{:S(2)}) copy-start(f32[192]{0:T(256)} %param.13) | copy-start | bytes 2308
  166.7 101.4 %reduce-scatter.5.cloned.1.call-start = ((), (), s32[]{:S(2)}) async-start(), calls=%async_computation.5 | async-start | bytes 1769472 | tf_op jit(solution)/shard_map/reduce_scatter | solution.py:59
  166.9 12.2 %collective-permute-start.2 = (bf16[192,16]{1,0:T(8,128)(2,1)S(1)}, bf16[192,16]{1,0:T(8,128)(2,1)S(1)}, u32[]{:S(2)}, u32[]{:S(2)}) collective-permute-start(bf16[192,16]{1,0:T(8,128)(2,1)S(1)} %get-tuple-element.63), channel_id=1, source_target_pairs={{0,8},{8,16},{16,24},{24,32},{32,40},{40,48},{48,56},{56,64},{64,7... | collective-permute-start | bytes 18440 | tf_op jit(solution)/shard_map/ppermute | solution.py:17
  176.9 5.4 collective-permute-start.3
  182.5 5.8 copy-start.6
  188.5 0.7 copy-start.9
  188.5 1.1 copy-start.12
  193.5 2.9 copy-start.23
  198.3 19.6 %copy-start.8 = (bf16[192,512]{1,0:T(8,128)(2,1)S(1)}, bf16[192,512]{1,0:T(8,128)(2,1)}, u32[]{:S(2)}) copy-start(bf16[192,512]{1,0:T(8,128)(2,1)} %param.15) | copy-start | bytes 589828
  200.9 20.1 %copy-start.2 = (bf16[192,512]{1,0:T(8,128)(2,1)S(1)}, bf16[192,512]{1,0:T(8,128)(2,1)}, u32[]{:S(2)}) copy-start(bf16[192,512]{1,0:T(8,128)(2,1)} %param.8) | copy-start | bytes 589828
  217.8 3.3 copy-start.3
  217.8 3.3 copy-start.7
  221.1 47.0 %copy-start.14 = (f32[192]{0:T(256)S(1)}, f32[192]{0:T(256)}, u32[]{:S(2)}) copy-start(f32[192]{0:T(256)} %param.9) | copy-start | bytes 2308
  221.1 64.1 %copy-start.4 = (f32[192,1536]{1,0:T(8,128)S(1)}, f32[192,1536]{1,0:T(8,128)}, u32[]{:S(2)}) copy-start(f32[192,1536]{1,0:T(8,128)} %convolution_multiply_fusion.2) | copy-start | bytes 3538948
  285.2 324.0 %copy-start.10 = (bf16[192,512]{1,0:T(8,128)(2,1)S(1)}, bf16[192,512]{1,0:T(8,128)(2,1)}, u32[]{:S(2)}) copy-start(bf16[192,512]{1,0:T(8,128)(2,1)} %reduce-scatter.5.cloned.1.call-done) | copy-start | bytes 589828
Sparse Core Ops, SparseCore 0:
  40.7 55.4 all-gather.2
  99.0 48.3 reduce-scatter.2
  166.8 50.9 all-gather.4
  220.5 47.5 reduce-scatter.4
where the time goes:
time: 621 us; the launch traced here: 617 us
  blocking collectives  414 us (67%)
  waiting for transfers between devices  122 us (20%)
  other arithmetic  29 us (5%)
  starting transfers between devices  20.4 us (3%)
  matrix products  16.4 us (3%)
  between operations  14.2 us (2%)
    psum x1, blocking collectives, local(): lax.psum((grad_out, grad_kernel, grad_conv_gain, grad_value, grad_gate, g...  324 us
    psum x6, blocking collectives, row_sums(): return lax.psum(values, 'tp')  90 us
    all_gather x2, waiting for transfers between devices, spread_channels(): return lax.all_gather(values, 'tp', axis=0, tiled=True)  69.4 us
    reduce_scatter x2, waiting for transfers between devices, reduce_inputs(): lax.psum_scatter(rounded.astype(jnp.bfloat16), 'tp', scatter_dimension=0,...  46.3 us
    ppermute x2, starting transfers between devices, with_halo(): lax.ppermute(tail, axis, [(i, (i + 1) % count) for i in range(ends)])  16.2 us
  transfers between devices with their start and end apart: 8, of which 6 were waited for; matrix products, arithmetic and copies ran while one was open for 5% of the time, Pallas kernels for 0%

commit v1 on v0

v1 whole, which is shorter than its diff:
```python
import functools

import jax
import jax.numpy as jnp
from jax import lax
from jax.experimental import pallas as pl
from jax.experimental.pallas import tpu as pltpu
from jax.sharding import PartitionSpec as P

EPS = 1e-05
F32 = jnp.float32
BF16 = jnp.bfloat16
MESH = pl.DeviceIdType.MESH

TP = 8
SEQ = 64
NZ = 8
NY = 4
CH = 192
FR = 512
D = CH * TP
TAPS = 32
REACH = TAPS // 2
PAD = 128
WIDE = FR + 2 * PAD
HALF = CH // 2
ZR = HALF // 2
ZL = D // 4
SR = CH // NZ
BLK = 32
GAIN_CONV = TAPS
GAIN_NORM = TAPS + 1


def fold8(v):
    out = v[0:8]
    for i in range(8, v.shape[0], 8):
        out = out + v[i : i + 8]
    return out


def row_block(i, blk):
    return pl.ds(pl.multiple_of(i * blk, blk), blk)


def put_tile(ref, a, b):
    for j in range(4):
        ref[j : j + 1, :] = a[:, 128 * j : 128 * j + 128]
        ref[4 + j : 5 + j, :] = b[:, 128 * j : 128 * j + 128]


def tile_row(t):
    return jnp.concatenate([t[j : j + 1] for j in range(4)], axis=1)


def kernel(
    x_ref, par_ref, wv_ref, wg_ref, wo_ref, cot_ref,
    block_out, input_grad, gval_out, ggate_out, gout_out, small_out,
    hat_in, value, sig, conv, hatc, dact, dglu,
    normed, act_all, da_s, da_r, dn_s, dn_r,
    glu_w, dcv_w, dv_b, dg_b, prod,
    st_s, st_r,
    g16, c1, s16, zr, y16, yr, r16,
    sm_s, sm_c, sm_t, sm_z, sm_y, sm_r,
    st_ss, st_rs, ag_ss, ag_rs, rs_ss, rs_rs, ha_ss, ha_rs,
    c1_ss, c1_rs, z_ss, z_rs, y_ss, y_rs, w_ss, w_rs, f_ss, f_rs,
    sc_ss, sc_rs, sz_ss, sz_rs, sy_ss, sy_rs, sw_ss, sw_rs,
):
    p = lax.axis_index("tp")
    q = lax.axis_index("seq")
    core = lax.rem(q, 2)
    chip = q // 2
    z = lax.rem(chip, NZ)
    yh = chip // NZ
    scale = float(FR * SEQ) ** (-0.5)
    sends = []

    def send(src, dst, ss, rs, dev):
        copy = pltpu.make_async_remote_copy(
            src_ref=src, dst_ref=dst, send_sem=ss, recv_sem=rs, device_id=dev, device_id_type=MESH
        )
        copy.start()
        sends.append(copy)

    def arrived(dst, ss, rs, dev):
        pltpu.make_async_remote_copy(
            src_ref=dst, dst_ref=dst, send_sem=ss, recv_sem=rs, device_id=dev, device_id_type=MESH
        ).wait_recv()

    def tp_dev(k):
        return {"tp": lax.rem(p + k, TP), "seq": q}

    def z_dev(k):
        return {"tp": p, "seq": (yh * NZ + lax.rem(z + k, NZ)) * 2 + core}

    def y_dev(k):
        return {"tp": p, "seq": (lax.rem(yh + k, NY) * NZ + z) * 2 + core}

    mate = {"tp": p, "seq": chip * 2 + (1 - core)}
    right = {"tp": p, "seq": lax.rem(q + 1, SEQ)}
    left = {"tp": p, "seq": lax.rem(q + SEQ - 1, SEQ)}

    barrier = pltpu.get_barrier_semaphore()
    peers = [tp_dev(k) for k in range(1, TP)] + [z_dev(k) for k in range(1, NZ)]
    peers += [y_dev(k) for k in range(1, NY)] + [mate, right, left]
    for dev in peers:
        pl.semaphore_signal(barrier, inc=1, device_id=dev, device_id_type=MESH)

    zero8 = jnp.zeros((8, FR), F32)

    def loop(n, body, init):
        return lax.fori_loop(0, n, body, init)

    def collapse(v):
        return jnp.sum(v, axis=0, keepdims=True)

    def local_moments(ref, slot):
        total = loop(CH // BLK, lambda i, a: a + fold8(ref[row_block(i, BLK), :].astype(F32)), zero8)
        mean = collapse(total) / CH

        def body(i, a):
            c = ref[row_block(i, BLK), :].astype(F32) - mean
            return a + fold8(c * c)

        put_tile(st_s.at[slot], mean, collapse(loop(CH // BLK, body, zero8)))

    def share(slot):
        st_r[slot, p] = st_s[slot]
        for k in range(1, TP):
            send(st_s.at[slot], st_r.at[slot, p], st_ss.at[slot, k - 1], st_rs.at[slot, k - 1], tp_dev(k))

    def shared(slot):
        for k in range(1, TP):
            arrived(st_r.at[slot, lax.rem(p + TP - k, TP)], st_ss.at[slot, k - 1], st_rs.at[slot, k - 1], tp_dev(k))
        return [st_r[slot, j] for j in range(TP)]

    def merged(slot):
        parts = shared(slot)
        total = parts[0]
        for t in parts[1:]:
            total = total + t
        mean = total[0:4] / TP
        spread = total[4:8]
        for t in parts:
            off = t[0:4] - mean
            spread = spread + CH * (off * off)
        inverse = lax.rsqrt(spread / D + EPS)
        return tile_row(mean), tile_row(inverse)

    def summed(slot):
        parts = shared(slot)
        total = parts[0]
        for t in parts[1:]:
            total = total + t
        return tile_row(total[0:4]) / D, tile_row(total[4:8]) / D

    def gather_send(buf, n):
        for k in range(1, TP):
            send(buf.at[p], buf.at[p], ag_ss.at[n, k - 1], ag_rs.at[n, k - 1], tp_dev(k))

    def gather_wait(buf, n):
        for k in range(1, TP):
            arrived(buf.at[lax.rem(p + TP - k, TP)], ag_ss.at[n, k - 1], ag_rs.at[n, k - 1], tp_dev(k))

    def scatter_send(out, into, n):
        for k in range(1, TP):
            send(
                out.at[lax.rem(p + k, TP)], into.at[p], rs_ss.at[n, k - 1], rs_rs.at[n, k - 1], tp_dev(k)
            )

    def scatter_wait(into, n):
        for k in range(1, TP):
            arrived(into.at[lax.rem(p + TP - k, TP)], rs_ss.at[n, k - 1], rs_rs.at[n, k - 1], tp_dev(k))

    def halo_send(buf, n):
        send(buf.at[:, PAD : 2 * PAD], buf.at[:, PAD + FR : WIDE], ha_ss.at[n, 0], ha_rs.at[n, 0], left)
        send(buf.at[:, FR : FR + PAD], buf.at[:, 0:PAD], ha_ss.at[n, 1], ha_rs.at[n, 1], right)

    def halo_wait(buf, n):
        arrived(buf.at[:, PAD + FR : WIDE], ha_ss.at[n, 0], ha_rs.at[n, 0], left)
        arrived(buf.at[:, 0:PAD], ha_ss.at[n, 1], ha_rs.at[n, 1], right)

        @pl.when(q == 0)
        def _():
            buf[:, 0:PAD] = jnp.zeros((CH, PAD), buf.dtype)

        @pl.when(q == SEQ - 1)
        def _():
            buf[:, PAD + FR : WIDE] = jnp.zeros((CH, PAD), buf.dtype)

    def contract_rows(w, v):
        return lax.dot_general(w, v, (((0,), (0,)), ((), ())), preferred_element_type=F32)

    def contract_cols(a, b):
        return lax.dot_general(a, b, (((1,), (1,)), ((), ())), preferred_element_type=F32)

    local_moments(x_ref, 0)
    pl.semaphore_wait(barrier, len(peers))
    share(0)

    def dact_body(d, c):
        lanes = pl.ds(pl.multiple_of(d * (2 * CH), 128), 2 * CH)
        term = contract_rows(wo_ref[:, lanes], cot_ref[...]).astype(BF16)
        da_s[2 * d] = term[0:CH]
        da_s[2 * d + 1] = term[CH : 2 * CH]
        return c

    loop(TP // 2, dact_body, 0)

    mean_in, inv_in = merged(0)

    def norm_body(i, c):
        r = row_block(i, BLK)
        h = (x_ref[r, :].astype(F32) - mean_in) * inv_in
        hat_in[r, :] = h
        normed[p, r, :] = (h * par_ref[r, GAIN_NORM : GAIN_NORM + 1]).astype(BF16)
        return c

    loop(CH // BLK, norm_body, 0)
    gather_send(normed, 0)
    da_r[p] = da_s[p]
    scatter_send(da_s, da_r, 0)

    gather_wait(normed, 0)
    everything = normed[...].reshape(D, FR)
    value[...] = jnp.dot(wv_ref[...], everything, preferred_element_type=F32)
    sig[...] = jnp.dot(wg_ref[...], everything, preferred_element_type=F32)

    def glu_body(i, c):
        r = row_block(i, BLK)
        s = jax.nn.sigmoid(sig[r, :])
        sig[r, :] = s
        glu_w[r, PAD : PAD + FR] = (value[r, :] * s).astype(BF16)
        return c

    loop(CH // BLK, glu_body, 0)
    halo_send(glu_w, 0)
    halo_wait(glu_w, 0)

    def conv_body(i, c):
        r = row_block(i, 16)
        w = glu_w[r, :].astype(F32)
        taps = par_ref[r, 0:TAPS]
        acc = jnp.zeros((16, FR), F32)
        for k in range(TAPS):
            acc = acc + taps[:, k : k + 1] * pltpu.roll(w, (REACH - k) % WIDE, 1)[:, PAD : PAD + FR]
        conv[r, :] = acc
        return c

    loop(CH // 16, conv_body, 0)
    local_moments(conv, 1)
    share(1)

    scatter_wait(da_r, 0)

    def dsum_body(i, c):
        r = row_block(i, BLK)
        total = da_r[0, r, :].astype(F32)
        for j in range(1, TP):
            total = total + da_r[j, r, :].astype(F32)
        dact[r, :] = total
        return c

    loop(CH // BLK, dsum_body, 0)
    mean_c, inv_c = merged(1)

    def act_body(i, carry):
        a, b = carry
        r = row_block(i, BLK)
        h = (conv[r, :] - mean_c) * inv_c
        hatc[r, :] = h
        g = par_ref[r, GAIN_CONV : GAIN_CONV + 1]
        scaled = h * g
        s = jax.nn.sigmoid(scaled)
        act_all[p, r, :] = (scaled * s).astype(BF16)
        ds = dact[r, :] * (s + scaled * s * (1.0 - s))
        sm_s[r, GAIN_CONV : GAIN_CONV + 1] = jnp.sum(ds * h, axis=1, keepdims=True)
        e = ds * g
        dact[r, :] = e
        return a + fold8(e), b + fold8(e * h)

    sm_s[...] = jnp.zeros((CH, 128), F32)
    first, second = loop(CH // BLK, act_body, (zero8, zero8))
    put_tile(st_s.at[2], collapse(first), collapse(second))
    share(2)
    gather_send(act_all, 1)
    first, second = summed(2)

    def dconv_body(i, c):
        r = row_block(i, BLK)
        dcv_w[r, PAD : PAD + FR] = ((dact[r, :] - first - hatc[r, :] * second) * inv_c).astype(BF16)
        return c

    loop(CH // BLK, dconv_body, 0)
    halo_send(dcv_w, 1)
    halo_wait(dcv_w, 1)

    def back_body(i, c):
        r = row_block(i, 16)
        w = dcv_w[r, :].astype(F32)
        taps = par_ref[r, 0:TAPS]
        u = glu_w[r, PAD : PAD + FR].astype(F32)
        acc = jnp.zeros((16, FR), F32)
        for k in range(TAPS):
            moved = pltpu.roll(w, (k - REACH) % WIDE, 1)[:, PAD : PAD + FR]
            acc = acc + taps[:, k : k + 1] * moved
            m = u * moved
            prod[k, r, :] = (m[:, 0:128] + m[:, 128:256]) + (m[:, 256:384] + m[:, 384:512])
        s = sig[r, :]
        dv = acc * s
        dv_b[r, :] = dv.astype(BF16)
        dg_b[r, :] = (dv * value[r, :] * (1.0 - s)).astype(BF16)
        return c

    loop(CH // 16, back_body, 0)

    other = pl.ds(pl.multiple_of((1 - core) * HALF, HALF), HALF)
    mine = pl.ds(pl.multiple_of(core * HALF, HALF), HALF)

    def pair_send(g):
        send(g16.at[g, other, :], c1.at[g], c1_ss.at[g], c1_rs.at[g], mate)

    def weight_grad(g, left_ref, all_ref):
        g16[g] = contract_cols(left_ref[...], all_ref[...].reshape(D, FR)).astype(BF16)
        pair_send(g)

    weight_grad(0, dv_b, normed)
    weight_grad(1, dg_b, normed)

    def dn_body(d, c):
        lanes = pl.ds(pl.multiple_of(d * (2 * CH), 128), 2 * CH)
        term = contract_rows(wv_ref[:, lanes], dv_b[...]) + contract_rows(wg_ref[:, lanes], dg_b[...])
        term = term.astype(BF16)
        dn_s[2 * d] = term[0:CH]
        dn_s[2 * d + 1] = term[CH : 2 * CH]
        return c

    loop(TP // 2, dn_body, 0)
    dn_r[p] = dn_s[p]
    scatter_send(dn_s, dn_r, 1)

    def z_block(zz):
        return (
            pl.ds(pl.multiple_of((zz // 4) * ZR, 16), ZR),
            pl.ds(pl.multiple_of(lax.rem(zz, 4) * ZL, 128), ZL),
        )

    def z_send(g):
        arrived(c1.at[g], c1_ss.at[g], c1_rs.at[g], mate)
        s16[g] = (g16[g, mine, :].astype(F32) + c1[g].astype(F32)).astype(BF16)
        for k in range(1, NZ):
            rr, ll = z_block(lax.rem(z + k, NZ))
            send(s16.at[g, rr, ll], zr.at[g, z], z_ss.at[g, k - 1], z_rs.at[g, k - 1], z_dev(k))
        rr, ll = z_block(z)
        zr[g, z] = s16[g, rr, ll]

    def y_send(g):
        for k in range(1, NZ):
            arrived(zr.at[g, lax.rem(z + NZ - k, NZ)], z_ss.at[g, k - 1], z_rs.at[g, k - 1], z_dev(k))
        total = zr[g, 0].astype(F32)
        for j in range(1, NZ):
            total = total + zr[g, j].astype(F32)
        y16[g] = total.astype(BF16)
        yr[g, yh] = total.astype(BF16)
        for k in range(1, NY):
            send(y16.at[g], yr.at[g, yh], y_ss.at[g, k - 1], y_rs.at[g, k - 1], y_dev(k))

    outs = (gval_out, ggate_out, gout_out)

    def out_block(zz, cc):
        rr, ll = z_block(zz)
        return pl.ds(pl.multiple_of(cc * HALF + (zz // 4) * ZR, 16), ZR), ll

    def w_send(g):
        for k in range(1, NY):
            arrived(yr.at[g, lax.rem(yh + NY - k, NY)], y_ss.at[g, k - 1], y_rs.at[g, k - 1], y_dev(k))
        total = yr[g, 0].astype(F32)
        for j in range(1, NY):
            total = total + yr[g, j].astype(F32)
        r16[g] = (total * scale).astype(BF16)
        rr, ll = out_block(z, core)
        outs[g][rr, ll] = r16[g]
        for k in range(1, NZ):
            send(r16.at[g], outs[g].at[rr, ll], w_ss.at[g, k - 1], w_rs.at[g, k - 1], z_dev(k))
        send(r16.at[g], outs[g].at[rr, ll], f_ss.at[g, 0], f_rs.at[g, 0], mate)

    def f_send(g):
        for k in range(1, NZ):
            rr, ll = out_block(lax.rem(z + NZ - k, NZ), core)
            arrived(outs[g].at[rr, ll], w_ss.at[g, k - 1], w_rs.at[g, k - 1], z_dev(k))
            send(outs[g].at[rr, ll], outs[g].at[rr, ll], f_ss.at[g, k], f_rs.at[g, k], mate)

    def f_wait(g):
        for k in range(NZ):
            rr, ll = out_block(lax.rem(z + NZ - k, NZ), 1 - core)
            arrived(outs[g].at[rr, ll], f_ss.at[g, k], f_rs.at[g, k], mate)

    z_send(0)
    z_send(1)

    gather_wait(act_all, 1)
    act_flat = act_all[...].reshape(D, FR)
    value[...] = jnp.dot(wo_ref[...], act_flat, preferred_element_type=F32)
    weight_grad(2, cot_ref, act_all)

    def out_body(i, c):
        r = row_block(i, BLK)
        block_out[r, :] = (x_ref[r, :].astype(F32) + value[r, :]).astype(BF16)
        return c

    loop(CH // BLK, out_body, 0)

    for k in range(TAPS):
        sm_s[:, k : k + 1] = jnp.sum(prod[k], axis=1, keepdims=True)

    z_send(2)

    scatter_wait(dn_r, 1)

    def dnorm_body(i, carry):
        a, b = carry
        r = row_block(i, BLK)
        total = dn_r[0, r, :].astype(F32)
        for j in range(1, TP):
            total = total + dn_r[j, r, :].astype(F32)
        h = hat_in[r, :]
        sm_s[r, GAIN_NORM : GAIN_NORM + 1] = jnp.sum(total * h, axis=1, keepdims=True)
        e = total * par_ref[r, GAIN_NORM : GAIN_NORM + 1]
        dact[r, :] = e
        return a + fold8(e), b + fold8(e * h)

    first, second = loop(CH // BLK, dnorm_body, (zero8, zero8))
    put_tile(st_s.at[3], collapse(first), collapse(second))
    share(3)
    send(sm_s, sm_c, sc_ss.at[0], sc_rs.at[0], mate)

    y_send(0)
    y_send(1)

    first, second = summed(3)

    def grad_body(i, c):
        r = row_block(i, BLK)
        back = (dact[r, :] - first - hat_in[r, :] * second) * inv_in
        input_grad[r, :] = (cot_ref[r, :].astype(F32) + back).astype(BF16)
        return c

    loop(CH // BLK, grad_body, 0)

    arrived(sm_c, sc_ss.at[0], sc_rs.at[0], mate)
    sm_t[...] = sm_s[...] + sm_c[...]

    def sm_rows(zz):
        return pl.ds(pl.multiple_of(zz * SR, 8), SR)

    for k in range(1, NZ):
        send(sm_t.at[sm_rows(lax.rem(z + k, NZ)), :], sm_z.at[z], sz_ss.at[k - 1], sz_rs.at[k - 1], z_dev(k))
    sm_z[z] = sm_t[sm_rows(z), :]

    w_send(0)
    w_send(1)
    y_send(2)

    for k in range(1, NZ):
        arrived(sm_z.at[lax.rem(z + NZ - k, NZ)], sz_ss.at[k - 1], sz_rs.at[k - 1], z_dev(k))
    total = sm_z[0]
    for j in range(1, NZ):
        total = total + sm_z[j]
    sm_r[0] = total
    sm_y[yh] = total
    for k in range(1, NY):
        send(sm_r.at[0], sm_y.at[yh], sy_ss.at[k - 1], sy_rs.at[k - 1], y_dev(k))

    f_send(0)
    f_send(1)
    w_send(2)

    for k in range(1, NY):
        arrived(sm_y.at[lax.rem(yh + NY - k, NY)], sy_ss.at[k - 1], sy_rs.at[k - 1], y_dev(k))
    total = sm_y[0]
    for j in range(1, NY):
        total = total + sm_y[j]
    sm_r[1] = total * scale
    small_out[sm_rows(z), :] = total * scale
    for k in range(1, NZ):
        send(sm_r.at[1], small_out.at[sm_rows(z), :], sw_ss.at[k - 1], sw_rs.at[k - 1], z_dev(k))

    f_send(2)
    for k in range(1, NZ):
        arrived(small_out.at[sm_rows(lax.rem(z + NZ - k, NZ)), :], sw_ss.at[k - 1], sw_rs.at[k - 1], z_dev(k))
    for g in range(3):
        f_wait(g)
    for copy in sends:
        copy.wait_send()


def local(
    frames_in, norm_gain, value_weight, gate_weight, depth_kernel, conv_gain, out_weight, cotangent
):
    par = jnp.concatenate(
        [depth_kernel, conv_gain[:, None], norm_gain[:, None], jnp.zeros((CH, 128 - TAPS - 2), F32)], axis=1
    )
    act = jax.ShapeDtypeStruct((CH, FR), BF16)
    mat = jax.ShapeDtypeStruct((CH, D), BF16)
    vm = pltpu.VMEM
    dma = pltpu.SemaphoreType.DMA
    full = vm((CH, FR), F32)
    eight = vm((TP, CH, FR), BF16)
    wide = vm((CH, WIDE), BF16)
    block = vm((CH, FR), BF16)
    scratch = [full] * 7 + [eight] * 6 + [wide, wide, block, block, vm((TAPS, CH, 128), F32)]
    scratch += [vm((4, 8, 128), F32), vm((4, TP, 8, 128), F32)]
    scratch += [
        vm((3, CH, D), BF16),
        vm((3, HALF, D), BF16),
        vm((3, HALF, D), BF16),
        vm((3, NZ, ZR, ZL), BF16),
        vm((3, ZR, ZL), BF16),
        vm((3, NY, ZR, ZL), BF16),
        vm((3, ZR, ZL), BF16),
    ]
    small = vm((CH, 128), F32)
    scratch += [small, small, small, vm((NZ, SR, 128), F32), vm((NY, SR, 128), F32), vm((2, SR, 128), F32)]
    for shape in ((4, 7), (2, 7), (2, 7), (2, 2), (3,), (3, 7), (3, 3), (3, 7), (3, 8), (1,), (7,), (3,), (7,)):
        scratch += [dma(shape), dma(shape)]
    vmem = pl.BlockSpec(memory_space=pltpu.VMEM)
    block_out, input_grad, gval, ggate, gout, small_grads = pl.pallas_call(
        kernel,
        out_shape=(act, act, mat, mat, mat, jax.ShapeDtypeStruct((CH, 128), F32)),
        in_specs=[vmem] * 6,
        out_specs=(vmem,) * 6,
        scratch_shapes=scratch,
        compiler_params=pltpu.CompilerParams(
            collective_id=0, has_side_effects=True, vmem_limit_bytes=60 * 1024 * 1024
        ),
    )(frames_in, par, value_weight, gate_weight, out_weight, cotangent)
    return (
        block_out,
        input_grad,
        small_grads[:, GAIN_NORM],
        gval,
        ggate,
        small_grads[:, 0:TAPS],
        small_grads[:, GAIN_CONV],
        gout,
    )


def solution(mesh):
    return jax.shard_map(
        local,
        mesh=mesh,
        in_specs=(
            P("tp", "seq"),
            P("tp"),
            P("tp", None),
            P("tp", None),
            P("tp", None),
            P("tp"),
            P("tp", None),
            P("tp", "seq"),
        ),
        out_specs=(
            P("tp", "seq"),
            P("tp", "seq"),
            P("tp"),
            P("tp", None),
            P("tp", None),
            P("tp", None),
            P("tp"),
            P("tp", None),
        ),
        check_vma=False,
    )
```

time: 621 us -> 156 us (0.25)
  blocking collectives: 414 us -> 0 us
  Pallas kernels: 0 us -> 143 us
  waiting for transfers between devices: 122 us -> 0 us
  other arithmetic: 29 us -> 0.77 us
  starting transfers between devices: 20.4 us -> 0 us
  matrix products: 16.4 us -> 0 us
  between operations: 14.2 us -> 0.7 us
  local copies, waits for them, and re-layouts: 0.89 us -> 11.3 us
    psum x7 -> x0, blocking collectives: 414 us -> none  [the longest x1 324 us: local(): lax.psum((grad_out, grad_kernel, grad_conv_gain, grad_value, grad_gate, g...]
    pallas_call x0 -> x1, Pallas kernels: none -> 143 us  [local(): pl.pallas_call(kernel, out_shape=(act, act, mat, mat, mat, jax.ShapeDtype...]
    all_gather x2 -> x0, waiting for transfers between devices: 69.4 us -> none  [spread_channels(): return lax.all_gather(values, 'tp', axis=0, tiled=True)]
    reduce_scatter x2 -> x0, waiting for transfers between devices: 46.3 us -> none  [reduce_inputs(): lax.psum_scatter(rounded.astype(jnp.bfloat16), 'tp', scatter_dimension=0,...]
    ppermute x4 -> x0, starting transfers between devices: 20.2 us -> none  [the longest x2 16.2 us: with_halo(): lax.ppermute(tail, axis, [(i, (i + 1) % count) for i in range(ends)])]
    dot_general x9 -> x0, matrix products: 16.4 us -> none  [the longest x3 6.57 us: contract_cols(): lax.dot_general(left, right, (((1,), (1,)), ((), ())), preferred_element_...]
    reduce_sum x8 -> x0, other arithmetic: 15.2 us -> none  [the longest x2 5.64 us: split_norm(): mean = row_sums(jnp.sum(values, axis=0, keepdims=True)) / width]
    convert_element_type x7 -> x0, other arithmetic: 11.1 us -> none  [the longest x1 5.81 us: local(): d_gate = (d_glu * value * gate_sig * (1.0 - gate_sig)).astype(jnp.bfloat16)]
  transfers between devices with their start and end apart: 8 -> 0, of which waited for: 6 -> 0; matrix products, arithmetic and copies ran while one was open for 5% -> 0% of each run, Pallas kernels for 0% -> 0%
where the time goes in v1:
time: 156 us
  Pallas kernels  143 us (92%)
  local copies, waits for them, and re-layouts  11.3 us (7%)
    pallas_call x1, Pallas kernels, local(): pl.pallas_call(kernel, out_shape=(act, act, mat, mat, mat, jax.ShapeDtype...  143 us
    unnamed x21, local copies, waits for them, and re-layouts  9.21 us

profile of v1, /device:TPU:1, one launch (start us, length us, event | category | flops | bytes accessed | tf_op | source)
XLA Modules:
  0.0 155.9 jit_solution(1228428237797093329)
XLA Ops:
  0.6 0.0 copy-start.5
  0.7 0.1 pad.3.clone
  0.7 0.6 copy-done.5
  1.3 0.0 copy-start.4
  1.3 0.1 copy.20
  1.4 0.6 copy-done.4
  2.1 0.0 copy-start.6
  2.1 0.1 copy.18
  2.2 0.6 copy-done.6
  2.8 0.1 copy.19
  2.9 0.8 maximum_maximum_fusion.par_ref
  3.7 143.1 %shard_map.143 = (bf16[192,512]{1,0:T(8,128)(2,1)}, bf16[192,512]{1,0:T(8,128)(2,1)}, bf16[192,1536]{1,0:T(8,128)(2,1)}, bf16[192,1536]{1,0:T(8,128)(2,1)}, bf16...) custom-call(bf16[192,512]{1,0:T(8,128)(2,1)} %x_ref.1, f32[192,128]{1,0:T(8,128)} %maximum_maximum_fusion.par_ref, ...), custom_call_target="tpu_custom_call" | custom-call | tf_op jit(solution)/shard_map/pallas_call | solution.py:527
  146.8 0.0 copy-start
  146.8 0.0 copy-start.3
  146.8 1.8 %slice_reduce_fusion = (f32[192]{0:T(256)}, f32[192]{0:T(256)}) fusion(f32[192,128]{1,0:T(8,128)} %get-tuple-element.16), kind=kLoop, calls=%fused_computation.1 | loop fusion | bytes 3072 | tf_op jit(solution)/shard_map/slice | solution.py:544
  148.6 0.0 copy-done
  148.6 0.7 copy.21
  149.3 1.6 %copy.27 = bf16[192,512]{1,0:T(8,128)(2,1)} copy(bf16[192,512]{1,0:T(8,128)(2,1)} %get-tuple-element.46) | data formatting | bytes 393216
  150.9 1.6 %copy.28 = bf16[192,512]{1,0:T(8,128)(2,1)} copy(bf16[192,512]{1,0:T(8,128)(2,1)} %get-tuple-element.47) | data formatting | bytes 393216
  152.6 0.0 copy-done.3
  152.6 0.0 copy-start.2
  152.6 0.8 copy.29
  153.4 0.5 copy-done.2
  153.8 0.0 copy-start.1
  153.8 0.8 copy.30
  154.7 0.5 copy-done.1
  155.1 0.8 copy.31
  (1 shorter events, 0.0 us)
Async XLA Ops:
  0.6 0.7 copy-start.5
  1.3 0.8 copy-start.4
  2.1 0.7 copy-start.6
  146.8 1.9 %copy-start = (f32[192,128]{1,0:T(8,128)S(1)}, f32[192,128]{1,0:T(8,128)}, u32[]{:S(2)}) copy-start(f32[192,128]{1,0:T(8,128)} %get-tuple-element.16) | copy-start | bytes 294916
  146.8 5.8 %copy-start.3 = (bf16[192,1536]{1,0:T(8,128)(2,1)S(1)}, bf16[192,1536]{1,0:T(8,128)(2,1)}, u32[]{:S(2)}) copy-start(bf16[192,1536]{1,0:T(8,128)(2,1)} %get-tuple-element.49) | copy-start | bytes 1769476
  152.6 1.3 copy-start.2
  153.8 1.3 copy-start.1

commit v2 on v1

v2 whole, which is shorter than its diff:
```python
import functools

import jax
import jax.numpy as jnp
from jax import lax
from jax.experimental import pallas as pl
from jax.experimental.pallas import tpu as pltpu
from jax.sharding import PartitionSpec as P

EPS = 1e-05
F32 = jnp.float32
BF16 = jnp.bfloat16
MESH = pl.DeviceIdType.MESH

TP = 8
SEQ = 64
NZ = 8
NY = 4
CH = 192
FR = 512
D = CH * TP
TAPS = 32
REACH = TAPS // 2
PAD = 128
WIDE = FR + 2 * PAD
HALF = CH // 2
ZR = HALF // 2
ZL = D // 4
SR = CH // NZ
BLK = 32
VMEM_LIMIT = 63 * 1024 * 1024
GAIN_CONV = TAPS
GAIN_NORM = TAPS + 1


def fold8(v):
    out = v[0:8]
    for i in range(8, v.shape[0], 8):
        out = out + v[i : i + 8]
    return out


def row_block(i, blk):
    return pl.ds(pl.multiple_of(i * blk, blk), blk)


def put_tile(ref, a, b):
    for j in range(4):
        ref[j : j + 1, :] = a[:, 128 * j : 128 * j + 128]
        ref[4 + j : 5 + j, :] = b[:, 128 * j : 128 * j + 128]


def tile_row(t):
    return jnp.concatenate([t[j : j + 1] for j in range(4)], axis=1)


def kernel(
    x_hbm, ng_hbm, wv_hbm, wg_hbm, dk_hbm, cg_hbm, wo_hbm, cot_hbm,
    *rest,
):
    finals, landed, rest = rest[0:6], rest[6:12], rest[12:]
    block_out, input_grad, gval_out, ggate_out, gout_out, small_out = landed
    (
        x_ref, ng_ref, wv_ref, wg_ref, dk_ref, cg_ref, wo_ref, cot_ref, par_t, par_ref,
        hat_in, value, sig, conv, hatc, dact,
        normed, act_all, da_s, dn_s, rs_r,
        glu_w, dcv_w, dv_b, dg_b, prod,
        st_s, st_r,
        g16, c1, s16, zr, y16, yr, r16,
        sm_s, sm_c, sm_t, sm_z, sm_y, sm_r,
        ld, fin,
        st_ss, st_rs, ag_ss, ag_rs, rs_ss, rs_rs, ha_ss, ha_rs,
        c1_ss, c1_rs, z_ss, z_rs, y_ss, y_rs, w_ss, w_rs, f_ss, f_rs,
        sc_ss, sc_rs, sz_ss, sz_rs, sy_ss, sy_rs, sw_ss, sw_rs,
    ) = rest
    stores = [pltpu.make_async_copy(landed[i], finals[i], fin.at[i]) for i in range(6)]
    fetch = (
        (x_hbm, x_ref), (dk_hbm, dk_ref), (cg_hbm, cg_ref), (ng_hbm, ng_ref),
        (wo_hbm, wo_ref), (cot_hbm, cot_ref), (wv_hbm, wv_ref), (wg_hbm, wg_ref),
    )
    loads = [pltpu.make_async_copy(src, dst, ld.at[i]) for i, (src, dst) in enumerate(fetch)]
    for copy in loads:
        copy.start()
    p = lax.axis_index("tp")
    q = lax.axis_index("seq")
    core = lax.rem(q, 2)
    chip = q // 2
    z = lax.rem(chip, NZ)
    yh = chip // NZ
    scale = float(FR * SEQ) ** (-0.5)
    sends = []

    sems = {
        "st": (st_ss, st_rs), "ag": (ag_ss, ag_rs), "rs": (rs_ss, rs_rs), "ha": (ha_ss, ha_rs),
        "c1": (c1_ss, c1_rs), "z": (z_ss, z_rs), "y": (y_ss, y_rs), "w": (w_ss, w_rs), "f": (f_ss, f_rs),
        "sc": (sc_ss, sc_rs), "sz": (sz_ss, sz_rs), "sy": (sy_ss, sy_rs), "sw": (sw_ss, sw_rs),
    }

    def remote(src, dst, key, dev):
        out, into = sems[key[0]]
        return pltpu.make_async_remote_copy(
            src_ref=src, dst_ref=dst, send_sem=out.at[key[1:]], recv_sem=into.at[key[1:]],
            device_id=dev, device_id_type=MESH,
        )

    def send(src, dst, key, dev):
        copy = remote(src, dst, key, dev)
        copy.start()
        sends.append(copy)

    def arrived(dst, key, dev):
        remote(dst, dst, key, dev).wait_recv()

    tx, ty = p // 2, lax.rem(p, 2)

    def at_tp(dx, dy):
        return lax.rem(tx + dx, 4) * 2 + lax.rem(ty + dy, 2)

    def hop(dx, dy):
        return {"tp": at_tp(dx, dy), "seq": q}

    def half(h):
        return pl.ds(h * HALF, HALF)

    def tp_dev(k):
        return {"tp": lax.rem(p + k, TP), "seq": q}

    def z_dev(k):
        return {"tp": p, "seq": (yh * NZ + lax.rem(z + k, NZ)) * 2 + core}

    def y_dev(k):
        return {"tp": p, "seq": (lax.rem(yh + k, NY) * NZ + z) * 2 + core}

    mate = {"tp": p, "seq": chip * 2 + (1 - core)}
    right = {"tp": p, "seq": lax.rem(q + 1, SEQ)}
    left = {"tp": p, "seq": lax.rem(q + SEQ - 1, SEQ)}

    barrier = pltpu.get_barrier_semaphore()
    peers = [tp_dev(k) for k in range(1, TP)] + [z_dev(k) for k in range(1, NZ)]
    peers += [y_dev(k) for k in range(1, NY)] + [mate, right, left]
    for dev in peers:
        pl.semaphore_signal(barrier, inc=1, device_id=dev, device_id_type=MESH)

    zero8 = jnp.zeros((8, FR), F32)

    def loop(n, body, init):
        return lax.fori_loop(0, n, body, init)

    def collapse(v):
        return jnp.sum(v, axis=0, keepdims=True)

    def local_moments(ref, slot):
        total = loop(CH // BLK, lambda i, a: a + fold8(ref[row_block(i, BLK), :].astype(F32)), zero8)
        mean = collapse(total) / CH

        def body(i, a):
            c = ref[row_block(i, BLK), :].astype(F32) - mean
            return a + fold8(c * c)

        put_tile(st_s.at[slot], mean, collapse(loop(CH // BLK, body, zero8)))

    def share(slot):
        st_r[slot, p] = st_s[slot]
        for k in range(1, TP):
            send(st_s.at[slot], st_r.at[slot, p], ("st", slot, k - 1), tp_dev(k))

    def shared(slot):
        for k in range(1, TP):
            arrived(st_r.at[slot, lax.rem(p + TP - k, TP)], ("st", slot, k - 1), tp_dev(k))
        return [st_r[slot, j] for j in range(TP)]

    def merged(slot):
        parts = shared(slot)
        total = parts[0]
        for t in parts[1:]:
            total = total + t
        mean = total[0:4] / TP
        spread = total[4:8]
        for t in parts:
            off = t[0:4] - mean
            spread = spread + CH * (off * off)
        inverse = lax.rsqrt(spread / D + EPS)
        return tile_row(mean), tile_row(inverse)

    def summed(slot):
        parts = shared(slot)
        total = parts[0]
        for t in parts[1:]:
            total = total + t
        return tile_row(total[0:4]) / D, tile_row(total[4:8]) / D

    RIGHT, LEFT, SIDE = (1, 0), (3, 0), (0, 1)

    gather_plan = (
        ((0, 0), 0, RIGHT), ((0, 0), 1, RIGHT), ((0, 0), 1, LEFT), ((0, 0), 0, LEFT),
        ((0, 0), 0, SIDE), ((0, 0), 1, SIDE), ((3, 0), 0, RIGHT), ((1, 0), 1, LEFT),
        ((0, 1), 0, RIGHT), ((0, 1), 0, LEFT), ((3, 0), 1, SIDE), ((1, 0), 1, SIDE),
        ((2, 0), 1, SIDE), ((3, 1), 0, RIGHT),
    )

    def gather_put(buf, n, i):
        (dx, dy), h, to = gather_plan[i]
        piece = buf.at[at_tp(dx, dy), half(h), :]
        send(piece, piece, ("ag", n, i), hop(*to))

    def gather_got(buf, n, i):
        (dx, dy), h, to = gather_plan[i]
        piece = buf.at[at_tp(dx + 4 - to[0], dy + to[1]), half(h), :]
        arrived(piece, ("ag", n, i), hop(*to))

    def gather_send(buf, n):
        for i in (0, 2, 4, 1, 3, 5):
            gather_put(buf, n, i)

    def gather_relay(buf, n):
        gather_got(buf, n, 4)
        gather_put(buf, n, 8)
        gather_got(buf, n, 2)
        gather_put(buf, n, 7)
        gather_put(buf, n, 11)
        gather_got(buf, n, 0)
        gather_put(buf, n, 6)
        gather_put(buf, n, 9)
        gather_got(buf, n, 1)
        gather_put(buf, n, 10)

    def gather_last(buf, n):
        gather_got(buf, n, 7)
        gather_put(buf, n, 12)
        gather_got(buf, n, 8)
        gather_put(buf, n, 13)

    def gather_wait(buf, n):
        for i in (3, 5, 6, 9, 10, 11, 12, 13):
            gather_got(buf, n, i)

    scatter_plan = (
        ((3, 0), 0, LEFT), ((3, 0), 1, LEFT), ((1, 0), 1, RIGHT), ((1, 0), 0, RIGHT),
        ((0, 1), 0, SIDE), ((0, 1), 1, SIDE), ((2, 0), 0, LEFT), ((2, 0), 1, RIGHT),
        ((3, 1), 0, LEFT), ((1, 1), 0, RIGHT), ((3, 1), 1, SIDE), ((1, 1), 1, SIDE),
        ((2, 1), 1, SIDE), ((2, 1), 0, LEFT),
    )

    def scatter_put(buf, n, i, merge=()):
        (dx, dy), h, to = scatter_plan[i]
        d = at_tp(dx, dy)
        for m in merge:
            arrived(rs_r.at[n, m], ("rs", n, m), hop(*scatter_plan[m][2]))
        if merge:

            def body(j, c):
                r = pl.ds(pl.multiple_of(h * HALF + j * BLK, BLK), BLK)
                total = buf[d, r, :].astype(F32)
                for m in merge:
                    total = total + rs_r[n, m, row_block(j, BLK), :].astype(F32)
                buf[d, r, :] = total.astype(BF16)
                return c

            loop(HALF // BLK, body, 0)
        send(buf.at[d, half(h), :], rs_r.at[n, i], ("rs", n, i), hop(*to))

    def scatter_send(buf, n):
        for i in (13, 12, 9, 6, 10, 3, 11, 5):
            scatter_put(buf, n, i)

    def scatter_relay(buf, n):
        scatter_put(buf, n, 8, (13,))
        scatter_put(buf, n, 7, (12,))
        scatter_put(buf, n, 0, (6,))
        scatter_put(buf, n, 1, (10,))

    def scatter_last(buf, n):
        scatter_put(buf, n, 4, (8, 9))
        scatter_put(buf, n, 2, (7, 11))

    def scatter_wait(n):
        for m in range(6):
            arrived(rs_r.at[n, m], ("rs", n, m), hop(*scatter_plan[m][2]))

    def scatter_sum(buf, n, r, j, h):
        total = buf[p, r, :].astype(F32)
        for m in ((0, 3, 4), (1, 2, 5))[h]:
            total = total + rs_r[n, m, row_block(j, BLK), :].astype(F32)
        return total

    def halo_send(buf, n):
        send(buf.at[:, PAD : 2 * PAD], buf.at[:, PAD + FR : WIDE], ("ha", n, 0), left)
        send(buf.at[:, FR : FR + PAD], buf.at[:, 0:PAD], ("ha", n, 1), right)

    def halo_wait(buf, n):
        arrived(buf.at[:, PAD + FR : WIDE], ("ha", n, 0), left)
        arrived(buf.at[:, 0:PAD], ("ha", n, 1), right)

        @pl.when(q == 0)
        def _():
            buf[:, 0:PAD] = jnp.zeros((CH, PAD), buf.dtype)

        @pl.when(q == SEQ - 1)
        def _():
            buf[:, PAD + FR : WIDE] = jnp.zeros((CH, PAD), buf.dtype)

    def contract_rows(w, v):
        return lax.dot_general(w, v, (((0,), (0,)), ((), ())), preferred_element_type=F32)

    def contract_cols(a, b):
        return lax.dot_general(a, b, (((1,), (1,)), ((), ())), preferred_element_type=F32)

    for copy in loads[0:4]:
        copy.wait()
    par_t[...] = jnp.zeros((128, 2 * 128), F32)
    par_t[0:TAPS, 0:CH] = dk_ref[...]
    par_t[GAIN_CONV : GAIN_CONV + 1, 0:CH] = cg_ref[...]
    par_t[GAIN_NORM : GAIN_NORM + 1, 0:CH] = ng_ref[...]
    par_ref[...] = par_t[...].T[0:CH]

    local_moments(x_ref, 0)
    pl.semaphore_wait(barrier, len(peers))
    share(0)
    mean_in, inv_in = merged(0)

    def norm_body(i, c):
        r = row_block(i, BLK)
        h = (x_ref[r, :].astype(F32) - mean_in) * inv_in
        hat_in[r, :] = h
        normed[p, r, :] = (h * par_ref[r, GAIN_NORM : GAIN_NORM + 1]).astype(BF16)
        return c

    loop(CH // BLK, norm_body, 0)
    gather_send(normed, 0)

    loads[4].wait()
    loads[5].wait()
    def dact_body(d, c):
        lanes = pl.ds(pl.multiple_of(d * (2 * CH), 128), 2 * CH)
        term = contract_rows(wo_ref[:, lanes], cot_ref[...]).astype(BF16)
        da_s[2 * d] = term[0:CH]
        da_s[2 * d + 1] = term[CH : 2 * CH]
        return c

    loop(TP // 2, dact_body, 0)
    gather_relay(normed, 0)
    gather_last(normed, 0)
    scatter_send(da_s, 0)
    loads[6].wait()
    loads[7].wait()
    gather_wait(normed, 0)
    everything = normed[...].reshape(D, FR)
    value[...] = jnp.dot(wv_ref[...], everything, preferred_element_type=F32)
    sig[...] = jnp.dot(wg_ref[...], everything, preferred_element_type=F32)

    def glu_body(i, c):
        r = row_block(i, BLK)
        s = jax.nn.sigmoid(sig[r, :])
        sig[r, :] = s
        glu_w[r, PAD : PAD + FR] = (value[r, :] * s).astype(BF16)
        return c

    loop(CH // BLK, glu_body, 0)
    halo_send(glu_w, 0)
    scatter_relay(da_s, 0)
    halo_wait(glu_w, 0)

    def conv_body(i, c):
        r = row_block(i, 16)
        w = glu_w[r, :].astype(F32)
        taps = par_ref[r, 0:TAPS]
        acc = jnp.zeros((16, FR), F32)
        for k in range(TAPS):
            acc = acc + taps[:, k : k + 1] * pltpu.roll(w, (REACH - k) % WIDE, 1)[:, PAD : PAD + FR]
        conv[r, :] = acc
        return c

    lax.fori_loop(0, CH // 32, conv_body, 0)
    scatter_last(da_s, 0)
    lax.fori_loop(CH // 32, CH // 16, conv_body, 0)
    local_moments(conv, 1)
    share(1)

    scatter_wait(0)
    for h in range(2):

        def dsum_body(j, c):
            r = pl.ds(pl.multiple_of(h * HALF + j * BLK, BLK), BLK)
            dact[r, :] = scatter_sum(da_s, 0, r, j, h)
            return c

        loop(HALF // BLK, dsum_body, 0)
    mean_c, inv_c = merged(1)

    def act_body(i, carry):
        a, b = carry
        r = row_block(i, BLK)
        h = (conv[r, :] - mean_c) * inv_c
        hatc[r, :] = h
        g = par_ref[r, GAIN_CONV : GAIN_CONV + 1]
        scaled = h * g
        s = jax.nn.sigmoid(scaled)
        act_all[p, r, :] = (scaled * s).astype(BF16)
        ds = dact[r, :] * (s + scaled * s * (1.0 - s))
        sm_s[r, GAIN_CONV : GAIN_CONV + 1] = jnp.sum(ds * h, axis=1, keepdims=True)
        e = ds * g
        dact[r, :] = e
        return a + fold8(e), b + fold8(e * h)

    sm_s[...] = jnp.zeros((CH, 128), F32)
    first, second = loop(CH // BLK, act_body, (zero8, zero8))
    put_tile(st_s.at[2], collapse(first), collapse(second))
    share(2)
    gather_send(act_all, 1)
    first, second = summed(2)

    def dconv_body(i, c):
        r = row_block(i, BLK)
        dcv_w[r, PAD : PAD + FR] = ((dact[r, :] - first - hatc[r, :] * second) * inv_c).astype(BF16)
        return c

    loop(CH // BLK, dconv_body, 0)
    halo_send(dcv_w, 1)
    gather_relay(act_all, 1)
    halo_wait(dcv_w, 1)

    def back_body(i, c):
        r = row_block(i, 16)
        w = dcv_w[r, :].astype(F32)
        taps = par_ref[r, 0:TAPS]
        u = glu_w[r, PAD : PAD + FR].astype(F32)
        acc = jnp.zeros((16, FR), F32)
        for k in range(TAPS):
            moved = pltpu.roll(w, (k - REACH) % WIDE, 1)[:, PAD : PAD + FR]
            acc = acc + taps[:, k : k + 1] * moved
            m = u * moved
            prod[k, r, :] = (m[:, 0:128] + m[:, 128:256]) + (m[:, 256:384] + m[:, 384:512])
        s = sig[r, :]
        dv = acc * s
        dv_b[r, :] = dv.astype(BF16)
        dg_b[r, :] = (dv * value[r, :] * (1.0 - s)).astype(BF16)
        return c

    lax.fori_loop(0, CH // 32, back_body, 0)
    gather_last(act_all, 1)
    lax.fori_loop(CH // 32, CH // 16, back_body, 0)

    other = pl.ds(pl.multiple_of((1 - core) * HALF, HALF), HALF)
    mine = pl.ds(pl.multiple_of(core * HALF, HALF), HALF)

    def pair_send(g):
        send(g16.at[g, other, :], c1.at[g], ("c1", g), mate)

    def weight_grad(g, left_ref, all_ref):
        g16[g] = contract_cols(left_ref[...], all_ref[...].reshape(D, FR)).astype(BF16)
        pair_send(g)

    weight_grad(0, dv_b, normed)
    weight_grad(1, dg_b, normed)
    gather_wait(act_all, 1)
    weight_grad(2, cot_ref, act_all)

    def dn_body(d, c):
        lanes = pl.ds(pl.multiple_of(d * (2 * CH), 128), 2 * CH)
        term = contract_rows(wv_ref[:, lanes], dv_b[...]) + contract_rows(wg_ref[:, lanes], dg_b[...])
        term = term.astype(BF16)
        dn_s[2 * d] = term[0:CH]
        dn_s[2 * d + 1] = term[CH : 2 * CH]
        return c

    loop(TP // 2, dn_body, 0)
    scatter_send(dn_s, 1)

    def z_block(zz):
        return (
            pl.ds(pl.multiple_of((zz // 4) * ZR, 16), ZR),
            pl.ds(pl.multiple_of(lax.rem(zz, 4) * ZL, 128), ZL),
        )

    def chains(g):
        sign = 1 if g % 2 == 0 else NZ - 1
        return ((0, 4, sign), (1, 3, NZ - sign))

    def z_start(g):
        arrived(c1.at[g], ("c1", g), mate)
        s16[g] = (g16[g, mine, :].astype(F32) + c1[g].astype(F32)).astype(BF16)
        z_hop(g, 1)

    def z_got(g, i, sign):
        arrived(zr.at[g, i], ("z", g, i), z_dev(sign))
        return zr[g, i].astype(F32)

    def z_hop(g, step):
        for chain, n, sign in chains(g):
            if step <= n:
                rr, ll = z_block(lax.rem(z + sign * (n + 1 - step), NZ))
                i = chain * 4 + step - 1
                if step > 1:
                    s16[g, rr, ll] = (s16[g, rr, ll].astype(F32) + z_got(g, i - 1, sign)).astype(BF16)
                send(s16.at[g, rr, ll], zr.at[g, i], ("z", g, i), z_dev(sign))

    def y_send(g):
        rr, ll = z_block(z)
        total = s16[g, rr, ll].astype(F32)
        for chain, n, sign in chains(g):
            total = total + z_got(g, chain * 4 + n - 1, sign)
        y16[g] = total.astype(BF16)
        yr[g, yh] = total.astype(BF16)
        for k in range(1, NY):
            send(y16.at[g], yr.at[g, yh], ("y", g, k - 1), y_dev(k))

    outs = (gval_out, ggate_out, gout_out)

    def out_block(zz, cc):
        rr, ll = z_block(zz)
        return pl.ds(pl.multiple_of(cc * HALF + (zz // 4) * ZR, 16), ZR), ll

    def w_start(g):
        for k in range(1, NY):
            arrived(yr.at[g, lax.rem(yh + NY - k, NY)], ("y", g, k - 1), y_dev(k))
        total = yr[g, 0].astype(F32)
        for j in range(1, NY):
            total = total + yr[g, j].astype(F32)
        r16[g] = (total * scale).astype(BF16)
        rr, ll = out_block(z, core)
        outs[g][rr, ll] = r16[g]
        for chain, n, sign in chains(g):
            send(r16.at[g], outs[g].at[rr, ll], ("w", g, chain * 4), z_dev(sign))
        send(r16.at[g], outs[g].at[rr, ll], ("f", g, 0), mate)

    def w_hop(g, step):
        for chain, n, sign in chains(g):
            if step <= n + 1:
                i = chain * 4 + step - 2
                rr, ll = out_block(lax.rem(z + (NZ - sign) * (step - 1), NZ), core)
                piece = outs[g].at[rr, ll]
                arrived(piece, ("w", g, i), z_dev(sign))
                if step <= n:
                    send(piece, piece, ("w", g, i + 1), z_dev(sign))
                send(piece, piece, ("f", g, 1 + i), mate)

    def f_wait(g):
        rr, ll = out_block(z, 1 - core)
        arrived(outs[g].at[rr, ll], ("f", g, 0), mate)
        for chain, n, sign in chains(g):
            for step in range(2, n + 2):
                rr, ll = out_block(lax.rem(z + (NZ - sign) * (step - 1), NZ), 1 - core)
                arrived(outs[g].at[rr, ll], ("f", g, 1 + chain * 4 + step - 2), mate)

    z_start(0)
    z_start(1)

    value[...] = jnp.dot(wo_ref[...], act_all[...].reshape(D, FR), preferred_element_type=F32)
    z_hop(0, 2)
    z_hop(1, 2)
    z_start(2)

    def out_body(i, c):
        r = row_block(i, BLK)
        block_out[r, :] = (x_ref[r, :].astype(F32) + value[r, :]).astype(BF16)
        return c

    loop(CH // BLK, out_body, 0)
    stores[0].start()
    scatter_relay(dn_s, 1)
    z_hop(0, 3)
    z_hop(1, 3)
    z_hop(2, 2)

    for k in range(TAPS):
        sm_s[:, k : k + 1] = jnp.sum(prod[k], axis=1, keepdims=True)

    scatter_last(dn_s, 1)
    z_hop(0, 4)
    z_hop(1, 4)
    z_hop(2, 3)
    y_send(0)
    y_send(1)
    z_hop(2, 4)
    scatter_wait(1)

    carry = (zero8, zero8)
    for h in range(2):

        def dnorm_body(j, carry):
            a, b = carry
            r = pl.ds(pl.multiple_of(h * HALF + j * BLK, BLK), BLK)
            total = scatter_sum(dn_s, 1, r, j, h)
            hat = hat_in[r, :]
            sm_s[r, GAIN_NORM : GAIN_NORM + 1] = jnp.sum(total * hat, axis=1, keepdims=True)
            e = total * par_ref[r, GAIN_NORM : GAIN_NORM + 1]
            dact[r, :] = e
            return a + fold8(e), b + fold8(e * hat)

        carry = loop(HALF // BLK, dnorm_body, carry)
    first, second = carry
    put_tile(st_s.at[3], collapse(first), collapse(second))
    share(3)
    send(sm_s, sm_c, ("sc", 0), mate)

    y_send(2)
    first, second = summed(3)

    def grad_body(i, c):
        r = row_block(i, BLK)
        back = (dact[r, :] - first - hat_in[r, :] * second) * inv_in
        input_grad[r, :] = (cot_ref[r, :].astype(F32) + back).astype(BF16)
        return c

    loop(CH // BLK, grad_body, 0)
    stores[1].start()

    arrived(sm_c, ("sc", 0), mate)
    sm_t[...] = sm_s[...] + sm_c[...]

    def sm_rows(zz):
        return pl.ds(pl.multiple_of(zz * SR, 8), SR)

    for k in range(1, NZ):
        send(sm_t.at[sm_rows(lax.rem(z + k, NZ)), :], sm_z.at[z], ("sz", k - 1), z_dev(k))
    sm_z[z] = sm_t[sm_rows(z), :]

    w_start(0)
    w_start(1)
    w_hop(0, 2)
    w_hop(1, 2)
    w_start(2)

    for k in range(1, NZ):
        arrived(sm_z.at[lax.rem(z + NZ - k, NZ)], ("sz", k - 1), z_dev(k))
    total = sm_z[0]
    for j in range(1, NZ):
        total = total + sm_z[j]
    sm_r[0] = total
    sm_y[yh] = total
    for k in range(1, NY):
        send(sm_r.at[0], sm_y.at[yh], ("sy", k - 1), y_dev(k))

    w_hop(0, 3)
    w_hop(1, 3)
    w_hop(2, 2)
    w_hop(0, 4)
    w_hop(1, 4)
    w_hop(2, 3)

    for k in range(1, NY):
        arrived(sm_y.at[lax.rem(yh + NY - k, NY)], ("sy", k - 1), y_dev(k))
    total = sm_y[0]
    for j in range(1, NY):
        total = total + sm_y[j]
    sm_r[1] = total * scale
    small_out[sm_rows(z), :] = total * scale
    for k in range(1, NZ):
        send(sm_r.at[1], small_out.at[sm_rows(z), :], ("sw", k - 1), z_dev(k))

    w_hop(0, 5)
    w_hop(1, 5)
    w_hop(2, 4)
    w_hop(2, 5)
    for k in range(1, NZ):
        arrived(small_out.at[sm_rows(lax.rem(z + NZ - k, NZ)), :], ("sw", k - 1), z_dev(k))
    stores[5].start()
    for g in range(3):
        f_wait(g)
        stores[2 + g].start()
    for copy in sends:
        copy.wait_send()
    for copy in stores:
        copy.wait()


def copy_out(*refs):
    ins, outs, stage, small, sem = refs[0:6], refs[6:14], refs[14:19], refs[19], refs[20]
    loads = [pltpu.make_async_copy(ins[i], stage[i], sem.at[i]) for i in range(5)]
    stores = [pltpu.make_async_copy(stage[i], outs[i], sem.at[5 + i]) for i in range(5)]
    last = pltpu.make_async_copy(ins[5], small, sem.at[10])
    for copy in loads + [last]:
        copy.start()
    for i in range(5):
        loads[i].wait()
        stores[i].start()
    last.wait()
    cols = jnp.concatenate([small[...], jnp.zeros((2 * 128 - CH, 128), F32)], axis=0).T
    outs[5][...] = cols[0:TAPS, 0:CH]
    outs[6][...] = cols[GAIN_CONV : GAIN_CONV + 1, 0:CH]
    outs[7][...] = cols[GAIN_NORM : GAIN_NORM + 1, 0:CH]
    for copy in stores:
        copy.wait()


def local(
    frames_in, norm_gain, value_weight, gate_weight, depth_kernel, conv_gain, out_weight, cotangent
):
    act = jax.ShapeDtypeStruct((CH, FR), BF16)
    mat = jax.ShapeDtypeStruct((CH, D), BF16)
    row = jax.ShapeDtypeStruct((1, CH), F32)
    vm = pltpu.VMEM
    dma = pltpu.SemaphoreType.DMA
    full = vm((CH, FR), F32)
    eight = vm((TP, CH, FR), BF16)
    wide = vm((CH, WIDE), BF16)
    block = vm((CH, FR), BF16)
    weight = vm((CH, D), BF16)
    small = vm((CH, 128), F32)
    line = vm((1, CH), F32)
    scratch = [block, block, weight, weight, weight, small]
    scratch += [block, line, weight, weight, vm((TAPS, CH), F32), line, weight, block, vm((128, 256), F32), small] + [full] * 6 + [eight] * 4
    scratch += [vm((2, 14, HALF, FR), BF16), wide, wide, block, block, vm((TAPS, CH, 128), F32)]
    scratch += [vm((4, 8, 128), F32), vm((4, TP, 8, 128), F32)]
    scratch += [
        vm((3, CH, D), BF16),
        vm((3, HALF, D), BF16),
        vm((3, HALF, D), BF16),
        vm((3, 8, ZR, ZL), BF16),
        vm((3, ZR, ZL), BF16),
        vm((3, NY, ZR, ZL), BF16),
        vm((3, ZR, ZL), BF16),
    ]
    scratch += [small, small, small, vm((NZ, SR, 128), F32), vm((NY, SR, 128), F32), vm((2, SR, 128), F32)]
    scratch += [dma((8,)), dma((6,))]
    for shape in ((4, 7), (2, 14), (2, 14), (2, 2), (3,), (3, 8), (3, 3), (3, 8), (3, 8), (1,), (7,), (3,), (7,)):
        scratch += [dma(shape), dma(shape)]
    vmem = pl.BlockSpec(memory_space=pltpu.VMEM)
    anywhere = pl.BlockSpec(memory_space=pl.ANY)
    results = pl.pallas_call(
        kernel,
        out_shape=(act, act, mat, mat, mat, jax.ShapeDtypeStruct((CH, 128), F32)),
        in_specs=[anywhere] * 8,
        out_specs=(anywhere,) * 6,
        scratch_shapes=scratch,
        compiler_params=pltpu.CompilerParams(
            collective_id=0, has_side_effects=True, vmem_limit_bytes=VMEM_LIMIT
        ),
    )(
        frames_in,
        norm_gain.reshape(1, CH),
        value_weight,
        gate_weight,
        depth_kernel.T,
        conv_gain.reshape(1, CH),
        out_weight,
        cotangent,
    )
    block_out, input_grad, gval, ggate, gout, gkernel, gconv, gnorm = pl.pallas_call(
        copy_out,
        out_shape=(act, act, mat, mat, mat, jax.ShapeDtypeStruct((TAPS, CH), F32), row, row),
        in_specs=[anywhere] * 6,
        out_specs=(anywhere,) * 5 + (vmem,) * 3,
        scratch_shapes=[block, block, weight, weight, weight, small, dma((11,))],
    )(*results)
    return (
        block_out,
        input_grad,
        gnorm.reshape(CH),
        gval,
        ggate,
        gkernel.T,
        gconv.reshape(CH),
        gout,
    )


def solution(mesh):
    return jax.shard_map(
        local,
        mesh=mesh,
        in_specs=(
            P("tp", "seq"),
            P("tp"),
            P("tp", None),
            P("tp", None),
            P("tp", None),
            P("tp"),
            P("tp", None),
            P("tp", "seq"),
        ),
        out_specs=(
            P("tp", "seq"),
            P("tp", "seq"),
            P("tp"),
            P("tp", None),
            P("tp", None),
            P("tp", None),
            P("tp"),
            P("tp", None),
        ),
        check_vma=False,
    )
```

time: 156 us -> 119 us (0.76)
  Pallas kernels: 143 us -> 118 us
  local copies, waits for them, and re-layouts: 11.3 us -> 0 us
    pallas_call x1, Pallas kernels: 143 us -> 115 us  [local(): pl.pallas_call(kernel, out_shape=(act, act, mat, mat, mat, jax.ShapeDtype...]
    unnamed x21 -> x0, local copies, waits for them, and re-layouts: 9.21 us -> none
    pallas_call x0 -> x1, Pallas kernels: none -> 3.19 us  [local(): pl.pallas_call(copy_out, out_shape=(act, act, mat, mat, mat, jax.ShapeDty...]
    slice x1 -> x0, local copies, waits for them, and re-layouts: 1.83 us -> none  [local(): small_grads[:, GAIN_CONV]]
where the time goes in v2:
time: 119 us
  Pallas kernels  118 us (99%)
    pallas_call x1, Pallas kernels, local(): pl.pallas_call(kernel, out_shape=(act, act, mat, mat, mat, jax.ShapeDtype...  115 us
    pallas_call x1, Pallas kernels, local(): pl.pallas_call(copy_out, out_shape=(act, act, mat, mat, mat, jax.ShapeDty...  3.19 us

profile of v2, /device:TPU:1, one launch (start us, length us, event | category | flops | bytes accessed | tf_op | source)
XLA Modules:
  0.0 118.8 jit_solution(9000566182628175413)
XLA Ops:
  0.6 115.0 %shard_map.143 = (bf16[192,512]{1,0:T(8,128)(2,1)}, bf16[192,512]{1,0:T(8,128)(2,1)}, bf16[192,1536]{1,0:T(8,128)(2,1)}, bf16[192,1536]{1,0:T(8,128)(2,1)}, bf16...) custom-call(bf16[192,512]{1,0:T(8,128)(2,1)} %x_hbm.1, f32[1,192]{1,0:T(1,128)} %bitcast.7, bf16[192,1536]{1,0:T(8,128)(2,1)} %wv_hbm.1, ...), custom_call_target="tpu_custom_call" | custom-call | tf_op jit(solution)/shard_map/pallas_call | solution.py:720
  115.6 3.2 %shard_map.144 = (bf16[192,512]{1,0:T(8,128)(2,1)}, bf16[192,512]{1,0:T(8,128)(2,1)}, bf16[192,1536]{1,0:T(8,128)(2,1)}, bf16[192,1536]{1,0:T(8,128)(2,1)}, bf16...) custom-call(bf16[192,512]{1,0:T(8,128)(2,1)} %get-tuple-element.22.refs_0_, ...), custom_call_target="tpu_custom_call" | custom-call | tf_op jit(solution)/shard_map/pallas_call | solution.py:739

commit v3 on v2

--- a/solution.py
+++ b/solution.py
@@ -58,30 +58,30 @@
     x_hbm, ng_hbm, wv_hbm, wg_hbm, dk_hbm, cg_hbm, wo_hbm, cot_hbm,
     *rest,
 ):
-    finals, landed, rest = rest[0:6], rest[6:12], rest[12:]
-    block_out, input_grad, gval_out, ggate_out, gout_out, small_out = landed
+    finals, landed, rest = rest[0:7], rest[7:14], rest[14:]
+    block_out, input_grad, gval_out, ggate_out, gout_out, small_out, norm_out = landed
     (
-        x_ref, ng_ref, wv_ref, wg_ref, dk_ref, cg_ref, wo_ref, cot_ref, par_t, par_ref,
+        ng_ref, wv_ref, wg_ref, dk_ref, cg_ref, wo_ref, cot_ref, par_t, par_ref,
         hat_in, value, sig, conv, hatc, dact,
-        normed, act_all, da_s, dn_s, rs_r,
+        x_all, gains_t, gains, st0_s, st0_r, normed, act_all, da_s, dn_s, rs_r,
         glu_w, dcv_w, dv_b, dg_b, prod,
         st_s, st_r,
         g16, c1, s16, zr, y16, yr, r16,
-        sm_s, sm_c, sm_t, sm_z, sm_y, sm_r,
+        ncol, nt_s, nt_z, nt_y, nt_c, sm_s, sm_c, sm_t, sm_z, sm_y, sm_r,
         ld, fin,
         st_ss, st_rs, ag_ss, ag_rs, rs_ss, rs_rs, ha_ss, ha_rs,
         c1_ss, c1_rs, z_ss, z_rs, y_ss, y_rs, w_ss, w_rs, f_ss, f_rs,
-        sc_ss, sc_rs, sz_ss, sz_rs, sy_ss, sy_rs, sw_ss, sw_rs,
+        nz_ss, nz_rs, ny_ss, ny_rs, nc_ss, nc_rs, sc_ss, sc_rs, sz_ss, sz_rs, sy_ss, sy_rs, sw_ss, sw_rs,
     ) = rest
-    stores = [pltpu.make_async_copy(landed[i], finals[i], fin.at[i]) for i in range(6)]
+    stores = [pltpu.make_async_copy(landed[i], finals[i], fin.at[i]) for i in range(7)]
+    p = lax.axis_index("tp")
     fetch = (
-        (x_hbm, x_ref), (dk_hbm, dk_ref), (cg_hbm, cg_ref), (ng_hbm, ng_ref),
+        (x_hbm, x_all.at[p]), (dk_hbm, dk_ref), (cg_hbm, cg_ref), (ng_hbm, ng_ref),
         (wo_hbm, wo_ref), (cot_hbm, cot_ref), (wv_hbm, wv_ref), (wg_hbm, wg_ref),
     )
     loads = [pltpu.make_async_copy(src, dst, ld.at[i]) for i, (src, dst) in enumerate(fetch)]
     for copy in loads:
         copy.start()
-    p = lax.axis_index("tp")
     q = lax.axis_index("seq")
     core = lax.rem(q, 2)
     chip = q // 2
@@ -93,7 +93,7 @@
     sems = {
         "st": (st_ss, st_rs), "ag": (ag_ss, ag_rs), "rs": (rs_ss, rs_rs), "ha": (ha_ss, ha_rs),
         "c1": (c1_ss, c1_rs), "z": (z_ss, z_rs), "y": (y_ss, y_rs), "w": (w_ss, w_rs), "f": (f_ss, f_rs),
-        "sc": (sc_ss, sc_rs), "sz": (sz_ss, sz_rs), "sy": (sy_ss, sy_rs), "sw": (sw_ss, sw_rs),
+        "nz": (nz_ss, nz_rs), "ny": (ny_ss, ny_rs), "nc": (nc_ss, nc_rs), "sc": (sc_ss, sc_rs), "sz": (sz_ss, sz_rs), "sy": (sy_ss, sy_rs), "sw": (sw_ss, sw_rs),
     }
 
     def remote(src, dst, key, dev):
@@ -149,15 +149,15 @@
     def collapse(v):
         return jnp.sum(v, axis=0, keepdims=True)
 
-    def local_moments(ref, slot):
-        total = loop(CH // BLK, lambda i, a: a + fold8(ref[row_block(i, BLK), :].astype(F32)), zero8)
+    def local_moments(rows, tile):
+        total = loop(CH // BLK, lambda i, a: a + fold8(rows(row_block(i, BLK))), zero8)
         mean = collapse(total) / CH
 
         def body(i, a):
-            c = ref[row_block(i, BLK), :].astype(F32) - mean
+            c = rows(row_block(i, BLK)) - mean
             return a + fold8(c * c)
 
-        put_tile(st_s.at[slot], mean, collapse(loop(CH // BLK, body, zero8)))
+        put_tile(tile, mean, collapse(loop(CH // BLK, body, zero8)))
 
     def share(slot):
         st_r[slot, p] = st_s[slot]
@@ -169,8 +169,7 @@
             arrived(st_r.at[slot, lax.rem(p + TP - k, TP)], ("st", slot, k - 1), tp_dev(k))
         return [st_r[slot, j] for j in range(TP)]
 
-    def merged(slot):
-        parts = shared(slot)
+    def merged(parts):
         total = parts[0]
         for t in parts[1:]:
             total = total + t
@@ -313,20 +312,15 @@
     par_t[GAIN_NORM : GAIN_NORM + 1, 0:CH] = ng_ref[...]
     par_ref[...] = par_t[...].T[0:CH]
 
-    local_moments(x_ref, 0)
+    local_moments(lambda r: x_all[p, r, :].astype(F32), st0_s)
+    st0_s[8:16, :] = jnp.zeros((8, 128), F32)
+    st0_s[8:9, :] = par_t[GAIN_NORM : GAIN_NORM + 1, 0:128]
+    st0_s[9:10, :] = par_t[GAIN_NORM : GAIN_NORM + 1, 128:256]
     pl.semaphore_wait(barrier, len(peers))
-    share(0)
-    mean_in, inv_in = merged(0)
-
-    def norm_body(i, c):
-        r = row_block(i, BLK)
-        h = (x_ref[r, :].astype(F32) - mean_in) * inv_in
-        hat_in[r, :] = h
-        normed[p, r, :] = (h * par_ref[r, GAIN_NORM : GAIN_NORM + 1]).astype(BF16)
-        return c
-
-    loop(CH // BLK, norm_body, 0)
-    gather_send(normed, 0)
+    st0_r[p] = st0_s[...]
+    for k in range(1, TP):
+        send(st0_s, st0_r.at[p], ("st", 0, k - 1), tp_dev(k))
+    gather_send(x_all, 0)
 
     loads[4].wait()
     loads[5].wait()
@@ -338,12 +332,42 @@
         return c
 
     loop(TP // 2, dact_body, 0)
-    gather_relay(normed, 0)
-    gather_last(normed, 0)
+    gather_relay(x_all, 0)
+    gather_last(x_all, 0)
+
+    for k in range(1, TP):
+        arrived(st0_r.at[lax.rem(p + TP - k, TP)], ("st", 0, k - 1), tp_dev(k))
+    gains_t[...] = jnp.zeros((128, 256), F32)
+    for j in range(TP):
+        gains_t[j : j + 1, 0:128] = st0_r[j, 8:9, :]
+        gains_t[j : j + 1, 128:256] = st0_r[j, 9:10, :]
+    gains[...] = gains_t[...].T
+    mean_in, inv_in = merged([st0_r[j] for j in range(TP)])
+
+    def own_body(i, c):
+        r = row_block(i, BLK)
+        h = (x_all[p, r, :].astype(F32) - mean_in) * inv_in
+        hat_in[r, :] = h
+        normed[p, r, :] = (h * par_ref[r, GAIN_NORM : GAIN_NORM + 1]).astype(BF16)
+        return c
+
+    loop(CH // BLK, own_body, 0)
     scatter_send(da_s, 0)
     loads[6].wait()
     loads[7].wait()
-    gather_wait(normed, 0)
+    gather_wait(x_all, 0)
+    for j in range(TP):
+
+        @pl.when(p != j)
+        def _():
+            def body(i, c):
+                r = row_block(i, BLK)
+                h = (x_all[j, r, :].astype(F32) - mean_in) * inv_in
+                normed[j, r, :] = (h * gains[r, j : j + 1]).astype(BF16)
+                return c
+
+            loop(CH // BLK, body, 0)
+
     everything = normed[...].reshape(D, FR)
     value[...] = jnp.dot(wv_ref[...], everything, preferred_element_type=F32)
     sig[...] = jnp.dot(wg_ref[...], everything, preferred_element_type=F32)
@@ -373,7 +397,7 @@
     lax.fori_loop(0, CH // 32, conv_body, 0)
     scatter_last(da_s, 0)
     lax.fori_loop(CH // 32, CH // 16, conv_body, 0)
-    local_moments(conv, 1)
+    local_moments(lambda r: conv[r, :], st_s.at[1])
     share(1)
 
     scatter_wait(0)
@@ -385,7 +409,7 @@
             return c
 
         loop(HALF // BLK, dsum_body, 0)
-    mean_c, inv_c = merged(1)
+    mean_c, inv_c = merged(shared(1))
 
     def act_body(i, carry):
         a, b = carry
@@ -452,19 +476,16 @@
 
     weight_grad(0, dv_b, normed)
     weight_grad(1, dg_b, normed)
-    gather_wait(act_all, 1)
-    weight_grad(2, cot_ref, act_all)
-
-    def dn_body(d, c):
-        lanes = pl.ds(pl.multiple_of(d * (2 * CH), 128), 2 * CH)
+
+    def dn_pair(dx, entries):
+        xx = lax.rem(tx + dx, 4)
+        lanes = pl.ds(pl.multiple_of(xx * (2 * CH), 128), 2 * CH)
         term = contract_rows(wv_ref[:, lanes], dv_b[...]) + contract_rows(wg_ref[:, lanes], dg_b[...])
         term = term.astype(BF16)
-        dn_s[2 * d] = term[0:CH]
-        dn_s[2 * d + 1] = term[CH : 2 * CH]
-        return c
-
-    loop(TP // 2, dn_body, 0)
-    scatter_send(dn_s, 1)
+        dn_s[2 * xx] = term[0:CH]
+        dn_s[2 * xx + 1] = term[CH : 2 * CH]
+        for i in entries:
+            scatter_put(dn_s, 1, i)
 
     def z_block(zz):
         return (
@@ -542,36 +563,55 @@
                 rr, ll = out_block(lax.rem(z + (NZ - sign) * (step - 1), NZ), 1 - core)
                 arrived(outs[g].at[rr, ll], ("f", g, 1 + chain * 4 + step - 2), mate)
 
+    dn_pair(2, (13, 12, 6))
+    dn_pair(1, (9, 3, 11))
     z_start(0)
     z_start(1)
-
-    value[...] = jnp.dot(wo_ref[...], act_all[...].reshape(D, FR), preferred_element_type=F32)
+    dn_pair(3, (10,))
+    dn_pair(0, (5,))
+    gather_wait(act_all, 1)
+    weight_grad(2, cot_ref, act_all)
     z_hop(0, 2)
     z_hop(1, 2)
+    scatter_relay(dn_s, 1)
     z_start(2)
+
+    for k in range(TAPS):
+        sm_s[:, k : k + 1] = jnp.sum(prod[k], axis=1, keepdims=True)
+    send(sm_s, sm_c, ("sc", 0), mate)
+
+    z_hop(0, 3)
+    z_hop(1, 3)
+    scatter_last(dn_s, 1)
+    z_hop(2, 2)
+
+    value[...] = jnp.dot(wo_ref[...], act_all[...].reshape(D, FR), preferred_element_type=F32)
 
     def out_body(i, c):
         r = row_block(i, BLK)
-        block_out[r, :] = (x_ref[r, :].astype(F32) + value[r, :]).astype(BF16)
+        block_out[r, :] = (x_all[p, r, :].astype(F32) + value[r, :]).astype(BF16)
         return c
 
+    z_hop(0, 4)
+    z_hop(1, 4)
     loop(CH // BLK, out_body, 0)
     stores[0].start()
-    scatter_relay(dn_s, 1)
-    z_hop(0, 3)
-    z_hop(1, 3)
-    z_hop(2, 2)
-
-    for k in range(TAPS):
-        sm_s[:, k : k + 1] = jnp.sum(prod[k], axis=1, keepdims=True)
-
-    scatter_last(dn_s, 1)
-    z_hop(0, 4)
-    z_hop(1, 4)
     z_hop(2, 3)
+
+    arrived(sm_c, ("sc", 0), mate)
+    sm_t[...] = sm_s[...] + sm_c[...]
+
+    def sm_rows(zz):
+        return pl.ds(pl.multiple_of(zz * SR, 8), SR)
+
+    for k in range(1, NZ):
+        send(sm_t.at[sm_rows(lax.rem(z + k, NZ)), :], sm_z.at[z], ("sz", k - 1), z_dev(k))
+    sm_z[z] = sm_t[sm_rows(z), :]
+
     y_send(0)
     y_send(1)
     z_hop(2, 4)
+    ncol[...] = jnp.zeros((256, 128), F32)
     scatter_wait(1)
 
     carry = (zero8, zero8)
@@ -582,7 +622,7 @@
             r = pl.ds(pl.multiple_of(h * HALF + j * BLK, BLK), BLK)
             total = scatter_sum(dn_s, 1, r, j, h)
             hat = hat_in[r, :]
-            sm_s[r, GAIN_NORM : GAIN_NORM + 1] = jnp.sum(total * hat, axis=1, keepdims=True)
+            ncol[r, 0:1] = jnp.sum(total * hat, axis=1, keepdims=True)
             e = total * par_ref[r, GAIN_NORM : GAIN_NORM + 1]
             dact[r, :] = e
             return a + fold8(e), b + fold8(e * hat)
@@ -591,9 +631,32 @@
     first, second = carry
     put_tile(st_s.at[3], collapse(first), collapse(second))
     share(3)
-    send(sm_s, sm_c, ("sc", 0), mate)
-
+
+    def all_sum(buf, count):
+        total = buf[0]
+        for j in range(1, count):
+            total = total + buf[j]
+        return total
+
+    flat = ncol[...].T
+    nt_s[0] = jnp.zeros((8, 128), F32)
+    nt_s[0, 0:1] = flat[0:1, 0:128]
+    nt_s[0, 1:2] = flat[0:1, 128:256]
+    nt_z[z] = nt_s[0]
+    for k in range(1, NZ):
+        send(nt_s.at[0], nt_z.at[z], ("nz", k - 1), z_dev(k))
     y_send(2)
+
+    for k in range(1, NZ):
+        arrived(sm_z.at[lax.rem(z + NZ - k, NZ)], ("sz", k - 1), z_dev(k))
+    total = all_sum(sm_z, NZ)
+    sm_r[0] = total
+    sm_y[yh] = total
+    for k in range(1, NY):
+        send(sm_r.at[0], sm_y.at[yh], ("sy", k - 1), y_dev(k))
+
+    w_start(0)
+    w_start(1)
     first, second = summed(3)
 
     def grad_body(i, c):
@@ -605,49 +668,37 @@
     loop(CH // BLK, grad_body, 0)
     stores[1].start()
 
-    arrived(sm_c, ("sc", 0), mate)
-    sm_t[...] = sm_s[...] + sm_c[...]
-
-    def sm_rows(zz):
-        return pl.ds(pl.multiple_of(zz * SR, 8), SR)
-
     for k in range(1, NZ):
-        send(sm_t.at[sm_rows(lax.rem(z + k, NZ)), :], sm_z.at[z], ("sz", k - 1), z_dev(k))
-    sm_z[z] = sm_t[sm_rows(z), :]
-
-    w_start(0)
-    w_start(1)
+        arrived(nt_z.at[lax.rem(z + NZ - k, NZ)], ("nz", k - 1), z_dev(k))
+    nt_s[1] = all_sum(nt_z, NZ)
+    nt_y[yh] = nt_s[1]
+    for k in range(1, NY):
+        send(nt_s.at[1], nt_y.at[yh], ("ny", k - 1), y_dev(k))
+
     w_hop(0, 2)
     w_hop(1, 2)
     w_start(2)
 
-    for k in range(1, NZ):
-        arrived(sm_z.at[lax.rem(z + NZ - k, NZ)], ("sz", k - 1), z_dev(k))
-    total = sm_z[0]
-    for j in range(1, NZ):
-        total = total + sm_z[j]
-    sm_r[0] = total
-    sm_y[yh] = total
-    for k in range(1, NY):
-        send(sm_r.at[0], sm_y.at[yh], ("sy", k - 1), y_dev(k))
-
-    w_hop(0, 3)
-    w_hop(1, 3)
-    w_hop(2, 2)
-    w_hop(0, 4)
-    w_hop(1, 4)
-    w_hop(2, 3)
-
     for k in range(1, NY):
         arrived(sm_y.at[lax.rem(yh + NY - k, NY)], ("sy", k - 1), y_dev(k))
-    total = sm_y[0]
-    for j in range(1, NY):
-        total = total + sm_y[j]
+    total = all_sum(sm_y, NY)
     sm_r[1] = total * scale
     small_out[sm_rows(z), :] = total * scale
     for k in range(1, NZ):
         send(sm_r.at[1], small_out.at[sm_rows(z), :], ("sw", k - 1), z_dev(k))
 
+    w_hop(0, 3)
+    w_hop(1, 3)
+    w_hop(2, 2)
+
+    for k in range(1, NY):
+        arrived(nt_y.at[lax.rem(yh + NY - k, NY)], ("ny", k - 1), y_dev(k))
+    nt_s[2] = all_sum(nt_y, NY)
+    send(nt_s.at[2], nt_c, ("nc", 0), mate)
+
+    w_hop(0, 4)
+    w_hop(1, 4)
+    w_hop(2, 3)
     w_hop(0, 5)
     w_hop(1, 5)
     w_hop(2, 4)
@@ -655,6 +706,9 @@
     for k in range(1, NZ):
         arrived(small_out.at[sm_rows(lax.rem(z + NZ - k, NZ)), :], ("sw", k - 1), z_dev(k))
     stores[5].start()
+    arrived(nt_c, ("nc", 0), mate)
+    norm_out[...] = (nt_s[2] + nt_c[...]) * scale
+    stores[6].start()
     for g in range(3):
         f_wait(g)
         stores[2 + g].start()
@@ -665,20 +719,22 @@
 
 
 def copy_out(*refs):
-    ins, outs, stage, small, sem = refs[0:6], refs[6:14], refs[14:19], refs[19], refs[20]
+    ins, outs, stage, small, norm, sem = refs[0:7], refs[7:15], refs[15:20], refs[20], refs[21], refs[22]
     loads = [pltpu.make_async_copy(ins[i], stage[i], sem.at[i]) for i in range(5)]
     stores = [pltpu.make_async_copy(stage[i], outs[i], sem.at[5 + i]) for i in range(5)]
-    last = pltpu.make_async_copy(ins[5], small, sem.at[10])
-    for copy in loads + [last]:
+    last = [pltpu.make_async_copy(ins[5], small, sem.at[10]), pltpu.make_async_copy(ins[6], norm, sem.at[11])]
+    for copy in last + loads:
         copy.start()
+    for copy in last:
+        copy.wait()
+    outs[7][:, 0:128] = norm[0:1, :]
+    outs[7][:, 128:CH] = norm[1:2, 0 : CH - 128]
     for i in range(5):
         loads[i].wait()
         stores[i].start()
-    last.wait()
     cols = jnp.concatenate([small[...], jnp.zeros((2 * 128 - CH, 128), F32)], axis=0).T
     outs[5][...] = cols[0:TAPS, 0:CH]
     outs[6][...] = cols[GAIN_CONV : GAIN_CONV + 1, 0:CH]
-    outs[7][...] = cols[GAIN_NORM : GAIN_NORM + 1, 0:CH]
     for copy in stores:
         copy.wait()
 
@@ -698,8 +754,11 @@
     weight = vm((CH, D), BF16)
     small = vm((CH, 128), F32)
     line = vm((1, CH), F32)
-    scratch = [block, block, weight, weight, weight, small]
-    scratch += [block, line, weight, weight, vm((TAPS, CH), F32), line, weight, block, vm((128, 256), F32), small] + [full] * 6 + [eight] * 4
+    tile = vm((8, 128), F32)
+    scratch = [block, block, weight, weight, weight, small, tile]
+    scratch += [line, weight, weight, vm((TAPS, CH), F32), line, weight, block, vm((128, 256), F32), small] + [full] * 6
+    scratch += [eight, vm((128, 256), F32), vm((256, 128), F32), vm((16, 128), F32), vm((TP, 16, 128), F32)]
+    scratch += [eight] * 4
     scratch += [vm((2, 14, HALF, FR), BF16), wide, wide, block, block, vm((TAPS, CH, 128), F32)]
     scratch += [vm((4, 8, 128), F32), vm((4, TP, 8, 128), F32)]
     scratch += [
@@ -711,17 +770,18 @@
         vm((3, NY, ZR, ZL), BF16),
         vm((3, ZR, ZL), BF16),
     ]
+    scratch += [vm((256, 128), F32), vm((3, 8, 128), F32), vm((NZ, 8, 128), F32), vm((NY, 8, 128), F32), tile]
     scratch += [small, small, small, vm((NZ, SR, 128), F32), vm((NY, SR, 128), F32), vm((2, SR, 128), F32)]
-    scratch += [dma((8,)), dma((6,))]
-    for shape in ((4, 7), (2, 14), (2, 14), (2, 2), (3,), (3, 8), (3, 3), (3, 8), (3, 8), (1,), (7,), (3,), (7,)):
+    scratch += [dma((8,)), dma((7,))]
+    for shape in ((4, 7), (2, 14), (2, 14), (2, 2), (3,), (3, 8), (3, 3), (3, 8), (3, 8), (7,), (3,), (1,), (1,), (7,), (3,), (7,)):
         scratch += [dma(shape), dma(shape)]
     vmem = pl.BlockSpec(memory_space=pltpu.VMEM)
     anywhere = pl.BlockSpec(memory_space=pl.ANY)
     results = pl.pallas_call(
         kernel,
-        out_shape=(act, act, mat, mat, mat, jax.ShapeDtypeStruct((CH, 128), F32)),
+        out_shape=(act, act, mat, mat, mat, jax.ShapeDtypeStruct((CH, 128), F32), jax.ShapeDtypeStruct((8, 128), F32)),
         in_specs=[anywhere] * 8,
-        out_specs=(anywhere,) * 6,
+        out_specs=(anywhere,) * 7,
         scratch_shapes=scratch,
         compiler_params=pltpu.CompilerParams(
             collective_id=0, has_side_effects=True, vmem_limit_bytes=VMEM_LIMIT
@@ -739,9 +799,9 @@
     block_out, input_grad, gval, ggate, gout, gkernel, gconv, gnorm = pl.pallas_call(
         copy_out,
         out_shape=(act, act, mat, mat, mat, jax.ShapeDtypeStruct((TAPS, CH), F32), row, row),
-        in_specs=[anywhere] * 6,
+        in_specs=[anywhere] * 7,
         out_specs=(anywhere,) * 5 + (vmem,) * 3,
-        scratch_shapes=[block, block, weight, weight, weight, small, dma((11,))],
+        scratch_shapes=[block, block, weight, weight, weight, small, tile, dma((12,))],
     )(*results)
     return (
         block_out,

time: 119 us -> 116 us (0.975)
  Pallas kernels: 118 us -> 115 us
    pallas_call x1, Pallas kernels: 115 us -> 111 us  [local(): pl.pallas_call(kernel, out_shape=(act, act, mat, mat, mat, jax.ShapeDtype...]
where the time goes in v3:
time: 116 us; the launch traced here: 115 us
  Pallas kernels  115 us (99%)
    pallas_call x1, Pallas kernels, local(): pl.pallas_call(kernel, out_shape=(act, act, mat, mat, mat, jax.ShapeDtype...  111 us
    pallas_call x1, Pallas kernels, local(): pl.pallas_call(copy_out, out_shape=(act, act, mat, mat, mat, jax.ShapeDty...  3.25 us

profile of v3, /device:TPU:1, one launch (start us, length us, event | category | flops | bytes accessed | tf_op | source)
XLA Modules:
  0.0 115.4 jit_solution(9627996277826879376)
XLA Ops:
  0.6 111.5 %shard_map.143 = (bf16[192,512]{1,0:T(8,128)(2,1)}, bf16[192,512]{1,0:T(8,128)(2,1)}, bf16[192,1536]{1,0:T(8,128)(2,1)}, bf16[192,1536]{1,0:T(8,128)(2,1)}, bf16...) custom-call(bf16[192,512]{1,0:T(8,128)(2,1)} %x_hbm.1, f32[1,192]{1,0:T(1,128)} %bitcast.7, ...), custom_call_target="tpu_custom_call" | custom-call | tf_op jit(solution)/shard_map/pallas_call | solution.py:780
  112.1 3.2 %shard_map.144 = (bf16[192,512]{1,0:T(8,128)(2,1)}, bf16[192,512]{1,0:T(8,128)(2,1)}, bf16[192,1536]{1,0:T(8,128)(2,1)}, bf16[192,1536]{1,0:T(8,128)(2,1)}, bf16...) custom-call(bf16[192,512]{1,0:T(8,128)(2,1)} %get-tuple-element.23.refs_0_, ...), custom_call_target="tpu_custom_call" | custom-call | tf_op jit(solution)/shard_map/pallas_call | solution.py:799

commit v4 on v3

--- a/solution.py
+++ b/solution.py
@@ -368,19 +368,18 @@
 
             loop(CH // BLK, body, 0)
 
-    everything = normed[...].reshape(D, FR)
-    value[...] = jnp.dot(wv_ref[...], everything, preferred_element_type=F32)
-    sig[...] = jnp.dot(wg_ref[...], everything, preferred_element_type=F32)
-
-    def glu_body(i, c):
-        r = row_block(i, BLK)
-        s = jax.nn.sigmoid(sig[r, :])
-        sig[r, :] = s
-        glu_w[r, PAD : PAD + FR] = (value[r, :] * s).astype(BF16)
-        return c
-
-    loop(CH // BLK, glu_body, 0)
+    def glu_part(low, high):
+        part = normed[:, :, low:high].reshape(D, high - low)
+        v = jnp.dot(wv_ref[...], part, preferred_element_type=F32)
+        s = jax.nn.sigmoid(jnp.dot(wg_ref[...], part, preferred_element_type=F32))
+        value[:, low:high] = v
+        sig[:, low:high] = s
+        glu_w[:, PAD + low : PAD + high] = (v * s).astype(BF16)
+
+    glu_part(0, 128)
+    glu_part(FR - 128, FR)
     halo_send(glu_w, 0)
+    glu_part(128, FR - 128)
     scatter_relay(da_s, 0)
     halo_wait(glu_w, 0)
 
@@ -388,10 +387,16 @@
         r = row_block(i, 16)
         w = glu_w[r, :].astype(F32)
         taps = par_ref[r, 0:TAPS]
-        acc = jnp.zeros((16, FR), F32)
-        for k in range(TAPS):
-            acc = acc + taps[:, k : k + 1] * pltpu.roll(w, (REACH - k) % WIDE, 1)[:, PAD : PAD + FR]
-        conv[r, :] = acc
+        spans = ((0, FR + PAD), (0, FR + PAD), (PAD, FR + PAD), (PAD, WIDE))
+        acc = [None] * 4
+        for b in range(8):
+            moved = pltpu.roll(w, WIDE - b, 1) if b else w
+            for a in range(4):
+                k = 8 * a + b
+                term = taps[:, k : k + 1] * moved[:, spans[a][0] : spans[a][1]]
+                acc[a] = term if acc[a] is None else acc[a] + term
+        total = acc[2] + pltpu.roll(acc[0], 16, 1)[:, PAD:] + pltpu.roll(acc[1], 8, 1)[:, PAD:]
+        conv[r, :] = total + pltpu.roll(acc[3], FR + PAD - 8, 1)[:, 0:FR]
         return c
 
     lax.fori_loop(0, CH // 32, conv_body, 0)
@@ -443,19 +448,35 @@
     gather_relay(act_all, 1)
     halo_wait(dcv_w, 1)
 
+    at_end = (q == SEQ - 1).astype(F32)
+
     def back_body(i, c):
         r = row_block(i, 16)
         w = dcv_w[r, :].astype(F32)
         taps = par_ref[r, 0:TAPS]
-        u = glu_w[r, PAD : PAD + FR].astype(F32)
-        acc = jnp.zeros((16, FR), F32)
-        for k in range(TAPS):
-            moved = pltpu.roll(w, (k - REACH) % WIDE, 1)[:, PAD : PAD + FR]
-            acc = acc + taps[:, k : k + 1] * moved
-            m = u * moved
-            prod[k, r, :] = (m[:, 0:128] + m[:, 128:256]) + (m[:, 256:384] + m[:, 384:512])
+        u = glu_w[r, :].astype(F32)
+        spans = ((PAD, WIDE), (PAD, WIDE), (PAD, FR + PAD), (0, FR + PAD))
+        glus = []
+        for a in range(4):
+            g = pltpu.roll(u, (16 - 8 * a) % WIDE, 1) if a != 2 else u
+            glus.append((g[:, PAD : PAD + FR], g[:, PAD + FR :] * at_end if a < 2 else None))
+        acc = [None] * 4
+        for b in range(8):
+            moved = pltpu.roll(w, b, 1) if b else w
+            for a in range(4):
+                k = 8 * a + b
+                term = taps[:, k : k + 1] * moved[:, spans[a][0] : spans[a][1]]
+                acc[a] = term if acc[a] is None else acc[a] + term
+                body, tail = glus[a]
+                m = body * moved[:, PAD : PAD + FR]
+                m = (m[:, 0:128] + m[:, 128:256]) + (m[:, 256:384] + m[:, 384:512])
+                if tail is not None and b:
+                    m = m + tail * moved[:, PAD + FR :]
+                prod[k, r, :] = m
+        total = acc[2] + pltpu.roll(acc[0], FR + PAD - 16, 1)[:, 0:FR]
+        total = total + pltpu.roll(acc[1], FR + PAD - 8, 1)[:, 0:FR] + pltpu.roll(acc[3], 8, 1)[:, PAD:]
         s = sig[r, :]
-        dv = acc * s
+        dv = total * s
         dv_b[r, :] = dv.astype(BF16)
         dg_b[r, :] = (dv * value[r, :] * (1.0 - s)).astype(BF16)
         return c
@@ -563,54 +584,33 @@
                 rr, ll = out_block(lax.rem(z + (NZ - sign) * (step - 1), NZ), 1 - core)
                 arrived(outs[g].at[rr, ll], ("f", g, 1 + chain * 4 + step - 2), mate)
 
-    dn_pair(2, (13, 12, 6))
-    dn_pair(1, (9, 3, 11))
+    gather_wait(act_all, 1)
+    weight_grad(2, cot_ref, act_all)
     z_start(0)
     z_start(1)
+    dn_pair(2, (13, 12, 6))
+    z_start(2)
+    dn_pair(1, (9, 3, 11))
+    z_hop(0, 2)
+    z_hop(1, 2)
     dn_pair(3, (10,))
     dn_pair(0, (5,))
-    gather_wait(act_all, 1)
-    weight_grad(2, cot_ref, act_all)
-    z_hop(0, 2)
-    z_hop(1, 2)
+    z_hop(2, 2)
+    z_hop(0, 3)
+    z_hop(1, 3)
     scatter_relay(dn_s, 1)
-    z_start(2)
+    z_hop(2, 3)
+    z_hop(0, 4)
+    z_hop(1, 4)
+    scatter_last(dn_s, 1)
+    z_hop(2, 4)
+    y_send(0)
+    y_send(1)
 
     for k in range(TAPS):
         sm_s[:, k : k + 1] = jnp.sum(prod[k], axis=1, keepdims=True)
     send(sm_s, sm_c, ("sc", 0), mate)
-
-    z_hop(0, 3)
-    z_hop(1, 3)
-    scatter_last(dn_s, 1)
-    z_hop(2, 2)
-
-    value[...] = jnp.dot(wo_ref[...], act_all[...].reshape(D, FR), preferred_element_type=F32)
-
-    def out_body(i, c):
-        r = row_block(i, BLK)
-        block_out[r, :] = (x_all[p, r, :].astype(F32) + value[r, :]).astype(BF16)
-        return c
-
-    z_hop(0, 4)
-    z_hop(1, 4)
-    loop(CH // BLK, out_body, 0)
-    stores[0].start()
-    z_hop(2, 3)
-
-    arrived(sm_c, ("sc", 0), mate)
-    sm_t[...] = sm_s[...] + sm_c[...]
-
-    def sm_rows(zz):
-        return pl.ds(pl.multiple_of(zz * SR, 8), SR)
-
-    for k in range(1, NZ):
-        send(sm_t.at[sm_rows(lax.rem(z + k, NZ)), :], sm_z.at[z], ("sz", k - 1), z_dev(k))
-    sm_z[z] = sm_t[sm_rows(z), :]
-
-    y_send(0)
-    y_send(1)
-    z_hop(2, 4)
+    y_send(2)
     ncol[...] = jnp.zeros((256, 128), F32)
     scatter_wait(1)
 
@@ -645,7 +645,51 @@
     nt_z[z] = nt_s[0]
     for k in range(1, NZ):
         send(nt_s.at[0], nt_z.at[z], ("nz", k - 1), z_dev(k))
-    y_send(2)
+
+    arrived(sm_c, ("sc", 0), mate)
+    sm_t[...] = sm_s[...] + sm_c[...]
+
+    def sm_rows(zz):
+        return pl.ds(pl.multiple_of(zz * SR, 8), SR)
+
+    for k in range(1, NZ):
+        send(sm_t.at[sm_rows(lax.rem(z + k, NZ)), :], sm_z.at[z], ("sz", k - 1), z_dev(k))
+    sm_z[z] = sm_t[sm_rows(z), :]
+
+    w_start(0)
+    w_start(1)
+    first, second = summed(3)
+
+    def grad_body(i, c):
+        r = row_block(i, BLK)
+        back = (dact[r, :] - first - hat_in[r, :] * second) * inv_in
+        input_grad[r, :] = (cot_ref[r, :].astype(F32) + back).astype(BF16)
+        return c
+
+    loop(CH // BLK, grad_body, 0)
+    stores[1].start()
+    w_hop(0, 2)
+    w_hop(1, 2)
+    w_start(2)
+
+    value[...] = jnp.dot(wo_ref[...], act_all[...].reshape(D, FR), preferred_element_type=F32)
+
+    def out_body(i, c):
+        r = row_block(i, BLK)
+        block_out[r, :] = (x_all[p, r, :].astype(F32) + value[r, :]).astype(BF16)
+        return c
+
+    loop(CH // BLK, out_body, 0)
+    stores[0].start()
+
+    w_hop(0, 3)
+    w_hop(1, 3)
+    for k in range(1, NZ):
+        arrived(nt_z.at[lax.rem(z + NZ - k, NZ)], ("nz", k - 1), z_dev(k))
+    nt_s[1] = all_sum(nt_z, NZ)
+    nt_y[yh] = nt_s[1]
+    for k in range(1, NY):
+        send(nt_s.at[1], nt_y.at[yh], ("ny", k - 1), y_dev(k))
 
     for k in range(1, NZ):
         arrived(sm_z.at[lax.rem(z + NZ - k, NZ)], ("sz", k - 1), z_dev(k))
@@ -655,29 +699,13 @@
     for k in range(1, NY):
         send(sm_r.at[0], sm_y.at[yh], ("sy", k - 1), y_dev(k))
 
-    w_start(0)
-    w_start(1)
-    first, second = summed(3)
-
-    def grad_body(i, c):
-        r = row_block(i, BLK)
-        back = (dact[r, :] - first - hat_in[r, :] * second) * inv_in
-        input_grad[r, :] = (cot_ref[r, :].astype(F32) + back).astype(BF16)
-        return c
-
-    loop(CH // BLK, grad_body, 0)
-    stores[1].start()
-
-    for k in range(1, NZ):
-        arrived(nt_z.at[lax.rem(z + NZ - k, NZ)], ("nz", k - 1), z_dev(k))
-    nt_s[1] = all_sum(nt_z, NZ)
-    nt_y[yh] = nt_s[1]
+    w_hop(2, 2)
+    w_hop(0, 4)
+    w_hop(1, 4)
     for k in range(1, NY):
-        send(nt_s.at[1], nt_y.at[yh], ("ny", k - 1), y_dev(k))
-
-    w_hop(0, 2)
-    w_hop(1, 2)
-    w_start(2)
+        arrived(nt_y.at[lax.rem(yh + NY - k, NY)], ("ny", k - 1), y_dev(k))
+    nt_s[2] = all_sum(nt_y, NY)
+    send(nt_s.at[2], nt_c, ("nc", 0), mate)
 
     for k in range(1, NY):
         arrived(sm_y.at[lax.rem(yh + NY - k, NY)], ("sy", k - 1), y_dev(k))
@@ -687,17 +715,6 @@
     for k in range(1, NZ):
         send(sm_r.at[1], small_out.at[sm_rows(z), :], ("sw", k - 1), z_dev(k))
 
-    w_hop(0, 3)
-    w_hop(1, 3)
-    w_hop(2, 2)
-
-    for k in range(1, NY):
-        arrived(nt_y.at[lax.rem(yh + NY - k, NY)], ("ny", k - 1), y_dev(k))
-    nt_s[2] = all_sum(nt_y, NY)
-    send(nt_s.at[2], nt_c, ("nc", 0), mate)
-
-    w_hop(0, 4)
-    w_hop(1, 4)
     w_hop(2, 3)
     w_hop(0, 5)
     w_hop(1, 5)

time: 116 us -> 116 us (level)
  no operation moved by 1% of the time
where the time goes in v4:
time: 116 us
  Pallas kernels  116 us (100%)
    pallas_call x1, Pallas kernels, local(): pl.pallas_call(kernel, out_shape=(act, act, mat, mat, mat, jax.ShapeDtype...  112 us
    pallas_call x1, Pallas kernels, local(): pl.pallas_call(copy_out, out_shape=(act, act, mat, mat, mat, jax.ShapeDty...  3.25 us

profile of v4, /device:TPU:1, one launch (start us, length us, event | category | flops | bytes accessed | tf_op | source)
XLA Modules:
  0.0 116.2 jit_solution(55345386287950264)
XLA Ops:
  0.6 112.3 %shard_map.143 = (bf16[192,512]{1,0:T(8,128)(2,1)}, bf16[192,512]{1,0:T(8,128)(2,1)}, bf16[192,1536]{1,0:T(8,128)(2,1)}, bf16[192,1536]{1,0:T(8,128)(2,1)}, bf16...) custom-call(bf16[192,512]{1,0:T(8,128)(2,1)} %x_hbm.1, f32[1,192]{1,0:T(1,128)} %bitcast.7, ...), custom_call_target="tpu_custom_call" | custom-call | tf_op jit(solution)/shard_map/pallas_call | solution.py:797
  113.0 3.2 %shard_map.144 = (bf16[192,512]{1,0:T(8,128)(2,1)}, bf16[192,512]{1,0:T(8,128)(2,1)}, bf16[192,1536]{1,0:T(8,128)(2,1)}, bf16[192,1536]{1,0:T(8,128)(2,1)}, bf16...) custom-call(bf16[192,512]{1,0:T(8,128)(2,1)} %get-tuple-element.23.refs_0_, ...), custom_call_target="tpu_custom_call" | custom-call | tf_op jit(solution)/shard_map/pallas_call | solution.py:816

commit v5 on v4

--- a/solution.py
+++ b/solution.py
@@ -600,17 +600,39 @@
     z_hop(1, 3)
     scatter_relay(dn_s, 1)
     z_hop(2, 3)
+
+    for k in range(TAPS):
+        sm_s[:, k : k + 1] = jnp.sum(prod[k], axis=1, keepdims=True)
+    send(sm_s, sm_c, ("sc", 0), mate)
+
     z_hop(0, 4)
     z_hop(1, 4)
     scatter_last(dn_s, 1)
     z_hop(2, 4)
     y_send(0)
     y_send(1)
-
-    for k in range(TAPS):
-        sm_s[:, k : k + 1] = jnp.sum(prod[k], axis=1, keepdims=True)
-    send(sm_s, sm_c, ("sc", 0), mate)
     y_send(2)
+
+    def sm_rows(zz):
+        return pl.ds(pl.multiple_of(zz * SR, 8), SR)
+
+    arrived(sm_c, ("sc", 0), mate)
+    sm_t[...] = sm_s[...] + sm_c[...]
+
+    for k in range(1, NZ):
+        send(sm_t.at[sm_rows(lax.rem(z + k, NZ)), :], sm_z.at[z], ("sz", k - 1), z_dev(k))
+    sm_z[z] = sm_t[sm_rows(z), :]
+
+    value[...] = jnp.dot(wo_ref[...], act_all[...].reshape(D, FR), preferred_element_type=F32)
+
+    def out_body(i, c):
+        r = row_block(i, BLK)
+        block_out[r, :] = (x_all[p, r, :].astype(F32) + value[r, :]).astype(BF16)
+        return c
+
+    loop(CH // BLK, out_body, 0)
+    stores[0].start()
+
     ncol[...] = jnp.zeros((256, 128), F32)
     scatter_wait(1)
 
@@ -646,51 +668,6 @@
     for k in range(1, NZ):
         send(nt_s.at[0], nt_z.at[z], ("nz", k - 1), z_dev(k))
 
-    arrived(sm_c, ("sc", 0), mate)
-    sm_t[...] = sm_s[...] + sm_c[...]
-
-    def sm_rows(zz):
-        return pl.ds(pl.multiple_of(zz * SR, 8), SR)
-
-    for k in range(1, NZ):
-        send(sm_t.at[sm_rows(lax.rem(z + k, NZ)), :], sm_z.at[z], ("sz", k - 1), z_dev(k))
-    sm_z[z] = sm_t[sm_rows(z), :]
-
-    w_start(0)
-    w_start(1)
-    first, second = summed(3)
-
-    def grad_body(i, c):
-        r = row_block(i, BLK)
-        back = (dact[r, :] - first - hat_in[r, :] * second) * inv_in
-        input_grad[r, :] = (cot_ref[r, :].astype(F32) + back).astype(BF16)
-        return c
-
-    loop(CH // BLK, grad_body, 0)
-    stores[1].start()
-    w_hop(0, 2)
-    w_hop(1, 2)
-    w_start(2)
-
-    value[...] = jnp.dot(wo_ref[...], act_all[...].reshape(D, FR), preferred_element_type=F32)
-
-    def out_body(i, c):
-        r = row_block(i, BLK)
-        block_out[r, :] = (x_all[p, r, :].astype(F32) + value[r, :]).astype(BF16)
-        return c
-
-    loop(CH // BLK, out_body, 0)
-    stores[0].start()
-
-    w_hop(0, 3)
-    w_hop(1, 3)
-    for k in range(1, NZ):
-        arrived(nt_z.at[lax.rem(z + NZ - k, NZ)], ("nz", k - 1), z_dev(k))
-    nt_s[1] = all_sum(nt_z, NZ)
-    nt_y[yh] = nt_s[1]
-    for k in range(1, NY):
-        send(nt_s.at[1], nt_y.at[yh], ("ny", k - 1), y_dev(k))
-
     for k in range(1, NZ):
         arrived(sm_z.at[lax.rem(z + NZ - k, NZ)], ("sz", k - 1), z_dev(k))
     total = all_sum(sm_z, NZ)
@@ -699,13 +676,28 @@
     for k in range(1, NY):
         send(sm_r.at[0], sm_y.at[yh], ("sy", k - 1), y_dev(k))
 
-    w_hop(2, 2)
-    w_hop(0, 4)
-    w_hop(1, 4)
+    w_start(0)
+    w_start(1)
+    w_start(2)
+    w_hop(0, 2)
+    w_hop(1, 2)
+
+    first, second = summed(3)
+
+    def grad_body(i, c):
+        r = row_block(i, BLK)
+        back = (dact[r, :] - first - hat_in[r, :] * second) * inv_in
+        input_grad[r, :] = (cot_ref[r, :].astype(F32) + back).astype(BF16)
+        return c
+
+    loop(CH // BLK, grad_body, 0)
+    stores[1].start()
+    for k in range(1, NZ):
+        arrived(nt_z.at[lax.rem(z + NZ - k, NZ)], ("nz", k - 1), z_dev(k))
+    nt_s[1] = all_sum(nt_z, NZ)
+    nt_y[yh] = nt_s[1]
     for k in range(1, NY):
-        arrived(nt_y.at[lax.rem(yh + NY - k, NY)], ("ny", k - 1), y_dev(k))
-    nt_s[2] = all_sum(nt_y, NY)
-    send(nt_s.at[2], nt_c, ("nc", 0), mate)
+        send(nt_s.at[1], nt_y.at[yh], ("ny", k - 1), y_dev(k))
 
     for k in range(1, NY):
         arrived(sm_y.at[lax.rem(yh + NY - k, NY)], ("sy", k - 1), y_dev(k))
@@ -715,10 +707,20 @@
     for k in range(1, NZ):
         send(sm_r.at[1], small_out.at[sm_rows(z), :], ("sw", k - 1), z_dev(k))
 
+    w_hop(2, 2)
+    w_hop(0, 3)
+    w_hop(1, 3)
     w_hop(2, 3)
+    w_hop(0, 4)
+    w_hop(1, 4)
+    for k in range(1, NY):
+        arrived(nt_y.at[lax.rem(yh + NY - k, NY)], ("ny", k - 1), y_dev(k))
+    nt_s[2] = all_sum(nt_y, NY)
+    send(nt_s.at[2], nt_c, ("nc", 0), mate)
+
+    w_hop(2, 4)
     w_hop(0, 5)
     w_hop(1, 5)
-    w_hop(2, 4)
     w_hop(2, 5)
     for k in range(1, NZ):
         arrived(small_out.at[sm_rows(lax.rem(z + NZ - k, NZ)), :], ("sw", k - 1), z_dev(k))

time: 116 us -> 112 us (0.966)
  Pallas kernels: 116 us -> 111 us
    pallas_call x1, Pallas kernels: 112 us -> 108 us  [local(): pl.pallas_call(kernel, out_shape=(act, act, mat, mat, mat, jax.ShapeDtype...]
where the time goes in v5:
time: 112 us
  Pallas kernels  111 us (99%)
    pallas_call x1, Pallas kernels, local(): pl.pallas_call(kernel, out_shape=(act, act, mat, mat, mat, jax.ShapeDtype...  108 us
    pallas_call x1, Pallas kernels, local(): pl.pallas_call(copy_out, out_shape=(act, act, mat, mat, mat, jax.ShapeDty...  3.25 us

profile of v5, /device:TPU:1, one launch (start us, length us, event | category | flops | bytes accessed | tf_op | source)
XLA Modules:
  0.0 111.7 jit_solution(17869751806287782887)
XLA Ops:
  0.6 107.9 %shard_map.143 = (bf16[192,512]{1,0:T(8,128)(2,1)}, bf16[192,512]{1,0:T(8,128)(2,1)}, bf16[192,1536]{1,0:T(8,128)(2,1)}, bf16[192,1536]{1,0:T(8,128)(2,1)}, bf16...) custom-call(bf16[192,512]{1,0:T(8,128)(2,1)} %x_hbm.1, f32[1,192]{1,0:T(1,128)} %bitcast.7, ...), custom_call_target="tpu_custom_call" | custom-call | tf_op jit(solution)/shard_map/pallas_call | solution.py:799
  108.5 3.2 %shard_map.144 = (bf16[192,512]{1,0:T(8,128)(2,1)}, bf16[192,512]{1,0:T(8,128)(2,1)}, bf16[192,1536]{1,0:T(8,128)(2,1)}, bf16[192,1536]{1,0:T(8,128)(2,1)}, bf16...) custom-call(bf16[192,512]{1,0:T(8,128)(2,1)} %get-tuple-element.23.refs_0_, ...), custom_call_target="tpu_custom_call" | custom-call | tf_op jit(solution)/shard_map/pallas_call | solution.py:818

commit v6 on v5

--- a/solution.py
+++ b/solution.py
@@ -28,7 +28,7 @@
 ZL = D // 4
 SR = CH // NZ
 BLK = 32
-VMEM_LIMIT = 63 * 1024 * 1024
+VMEM_LIMIT = 48 * 1024 * 1024
 GAIN_CONV = TAPS
 GAIN_NORM = TAPS + 1
 
@@ -58,7 +58,7 @@
     x_hbm, ng_hbm, wv_hbm, wg_hbm, dk_hbm, cg_hbm, wo_hbm, cot_hbm,
     *rest,
 ):
-    finals, landed, rest = rest[0:7], rest[7:14], rest[14:]
+    landed, rest = rest[0:7], rest[7:]
     block_out, input_grad, gval_out, ggate_out, gout_out, small_out, norm_out = landed
     (
         ng_ref, wv_ref, wg_ref, dk_ref, cg_ref, wo_ref, cot_ref, par_t, par_ref,
@@ -68,12 +68,11 @@
         st_s, st_r,
         g16, c1, s16, zr, y16, yr, r16,
         ncol, nt_s, nt_z, nt_y, nt_c, sm_s, sm_c, sm_t, sm_z, sm_y, sm_r,
-        ld, fin,
+        ld,
         st_ss, st_rs, ag_ss, ag_rs, rs_ss, rs_rs, ha_ss, ha_rs,
         c1_ss, c1_rs, z_ss, z_rs, y_ss, y_rs, w_ss, w_rs, f_ss, f_rs,
         nz_ss, nz_rs, ny_ss, ny_rs, nc_ss, nc_rs, sc_ss, sc_rs, sz_ss, sz_rs, sy_ss, sy_rs, sw_ss, sw_rs,
     ) = rest
-    stores = [pltpu.make_async_copy(landed[i], finals[i], fin.at[i]) for i in range(7)]
     p = lax.axis_index("tp")
     fetch = (
         (x_hbm, x_all.at[p]), (dk_hbm, dk_ref), (cg_hbm, cg_ref), (ng_hbm, ng_ref),
@@ -631,7 +630,6 @@
         return c
 
     loop(CH // BLK, out_body, 0)
-    stores[0].start()
 
     ncol[...] = jnp.zeros((256, 128), F32)
     scatter_wait(1)
@@ -691,7 +689,6 @@
         return c
 
     loop(CH // BLK, grad_body, 0)
-    stores[1].start()
     for k in range(1, NZ):
         arrived(nt_z.at[lax.rem(z + NZ - k, NZ)], ("nz", k - 1), z_dev(k))
     nt_s[1] = all_sum(nt_z, NZ)
@@ -724,33 +721,22 @@
     w_hop(2, 5)
     for k in range(1, NZ):
         arrived(small_out.at[sm_rows(lax.rem(z + NZ - k, NZ)), :], ("sw", k - 1), z_dev(k))
-    stores[5].start()
     arrived(nt_c, ("nc", 0), mate)
     norm_out[...] = (nt_s[2] + nt_c[...]) * scale
-    stores[6].start()
     for g in range(3):
         f_wait(g)
-        stores[2 + g].start()
     for copy in sends:
         copy.wait_send()
+
+
+def copy_out(*refs):
+    ins, outs, sem = refs[0:7], refs[7:15], refs[15]
+    small, norm = ins[5], ins[6]
+    stores = [pltpu.make_async_copy(ins[i], outs[i], sem.at[i]) for i in range(5)]
     for copy in stores:
-        copy.wait()
-
-
-def copy_out(*refs):
-    ins, outs, stage, small, norm, sem = refs[0:7], refs[7:15], refs[15:20], refs[20], refs[21], refs[22]
-    loads = [pltpu.make_async_copy(ins[i], stage[i], sem.at[i]) for i in range(5)]
-    stores = [pltpu.make_async_copy(stage[i], outs[i], sem.at[5 + i]) for i in range(5)]
-    last = [pltpu.make_async_copy(ins[5], small, sem.at[10]), pltpu.make_async_copy(ins[6], norm, sem.at[11])]
-    for copy in last + loads:
         copy.start()
-    for copy in last:
-        copy.wait()
     outs[7][:, 0:128] = norm[0:1, :]
     outs[7][:, 128:CH] = norm[1:2, 0 : CH - 128]
-    for i in range(5):
-        loads[i].wait()
-        stores[i].start()
     cols = jnp.concatenate([small[...], jnp.zeros((2 * 128 - CH, 128), F32)], axis=0).T
     outs[5][...] = cols[0:TAPS, 0:CH]
     outs[6][...] = cols[GAIN_CONV : GAIN_CONV + 1, 0:CH]
@@ -774,8 +760,7 @@
     small = vm((CH, 128), F32)
     line = vm((1, CH), F32)
     tile = vm((8, 128), F32)
-    scratch = [block, block, weight, weight, weight, small, tile]
-    scratch += [line, weight, weight, vm((TAPS, CH), F32), line, weight, block, vm((128, 256), F32), small] + [full] * 6
+    scratch = [line, weight, weight, vm((TAPS, CH), F32), line, weight, block, vm((128, 256), F32), small] + [full] * 6
     scratch += [eight, vm((128, 256), F32), vm((256, 128), F32), vm((16, 128), F32), vm((TP, 16, 128), F32)]
     scratch += [eight] * 4
     scratch += [vm((2, 14, HALF, FR), BF16), wide, wide, block, block, vm((TAPS, CH, 128), F32)]
@@ -791,36 +776,38 @@
     ]
     scratch += [vm((256, 128), F32), vm((3, 8, 128), F32), vm((NZ, 8, 128), F32), vm((NY, 8, 128), F32), tile]
     scratch += [small, small, small, vm((NZ, SR, 128), F32), vm((NY, SR, 128), F32), vm((2, SR, 128), F32)]
-    scratch += [dma((8,)), dma((7,))]
+    scratch += [dma((8,))]
     for shape in ((4, 7), (2, 14), (2, 14), (2, 2), (3,), (3, 8), (3, 3), (3, 8), (3, 8), (7,), (3,), (1,), (1,), (7,), (3,), (7,)):
         scratch += [dma(shape), dma(shape)]
     vmem = pl.BlockSpec(memory_space=pltpu.VMEM)
     anywhere = pl.BlockSpec(memory_space=pl.ANY)
+    hbm = pl.BlockSpec(memory_space=pltpu.HBM)
     results = pl.pallas_call(
         kernel,
         out_shape=(act, act, mat, mat, mat, jax.ShapeDtypeStruct((CH, 128), F32), jax.ShapeDtypeStruct((8, 128), F32)),
-        in_specs=[anywhere] * 8,
-        out_specs=(anywhere,) * 7,
+        in_specs=[hbm] * 8,
+        out_specs=(vmem,) * 7,
         scratch_shapes=scratch,
         compiler_params=pltpu.CompilerParams(
             collective_id=0, has_side_effects=True, vmem_limit_bytes=VMEM_LIMIT
         ),
     )(
-        frames_in,
-        norm_gain.reshape(1, CH),
-        value_weight,
-        gate_weight,
-        depth_kernel.T,
-        conv_gain.reshape(1, CH),
-        out_weight,
-        cotangent,
+        pltpu.with_memory_space_constraint(frames_in, pltpu.HBM),
+        pltpu.with_memory_space_constraint(norm_gain.reshape(1, CH), pltpu.HBM),
+        pltpu.with_memory_space_constraint(value_weight, pltpu.HBM),
+        pltpu.with_memory_space_constraint(gate_weight, pltpu.HBM),
+        pltpu.with_memory_space_constraint(depth_kernel.T, pltpu.HBM),
+        pltpu.with_memory_space_constraint(conv_gain.reshape(1, CH), pltpu.HBM),
+        pltpu.with_memory_space_constraint(out_weight, pltpu.HBM),
+        pltpu.with_memory_space_constraint(cotangent, pltpu.HBM),
     )
     block_out, input_grad, gval, ggate, gout, gkernel, gconv, gnorm = pl.pallas_call(
         copy_out,
         out_shape=(act, act, mat, mat, mat, jax.ShapeDtypeStruct((TAPS, CH), F32), row, row),
-        in_specs=[anywhere] * 7,
+        in_specs=[vmem] * 7,
         out_specs=(anywhere,) * 5 + (vmem,) * 3,
-        scratch_shapes=[block, block, weight, weight, weight, small, tile, dma((12,))],
+        scratch_shapes=[dma((5,))],
+        compiler_params=pltpu.CompilerParams(vmem_limit_bytes=8 * 1024 * 1024),
     )(*results)
     return (
         block_out,

time: 112 us -> 110 us (0.982)
  Pallas kernels: 111 us -> 109 us
    pallas_call x1, Pallas kernels: 3.25 us -> 2 us  [local(): pl.pallas_call(copy_out, out_shape=(act, act, mat, mat, mat, jax.ShapeDty...]
where the time goes in v6:
time: 110 us
  Pallas kernels  109 us (99%)
    pallas_call x1, Pallas kernels, local(): pl.pallas_call(kernel, out_shape=(act, act, mat, mat, mat, jax.ShapeDtype...  107 us

profile of v6, /device:TPU:1, one launch (start us, length us, event | category | flops | bytes accessed | tf_op | source)
XLA Modules:
  0.0 109.9 jit_solution(13543880306876075901)
XLA Ops:
  0.6 107.2 %shard_map.143 = (bf16[192,512]{1,0:T(8,128)(2,1)S(1)}, bf16[192,512]{1,0:T(8,128)(2,1)S(1)}, bf16[192,1536]{1,0:T(8,128)(2,1)S(1)}, bf16[192,1536]{1,0:T(8,128)...) custom-call(bf16[192,512]{1,0:T(8,128)(2,1)} %x_hbm.1, f32[1,192]{1,0:T(1,128)} %bitcast.7, ...), custom_call_target="tpu_custom_call" | custom-call | tf_op jit(solution)/shard_map/pallas_call | solution.py:785
  107.9 2.0 %shard_map.144 = (bf16[192,512]{1,0:T(8,128)(2,1)}, bf16[192,512]{1,0:T(8,128)(2,1)}, bf16[192,1536]{1,0:T(8,128)(2,1)}, bf16[192,1536]{1,0:T(8,128)(2,1)}, bf16...) custom-call(bf16[192,512]{1,0:T(8,128)(2,1)S(1)} %get-tuple-element.23.refs_0_, ...), custom_call_target="tpu_custom_call" | custom-call | tf_op jit(solution)/shard_map/pallas_call | solution.py:804

commit v7 on v6

--- a/solution.py
+++ b/solution.py
@@ -354,18 +354,27 @@
     scatter_send(da_s, 0)
     loads[6].wait()
     loads[7].wait()
-    gather_wait(x_all, 0)
-    for j in range(TP):
-
-        @pl.when(p != j)
-        def _():
-            def body(i, c):
-                r = row_block(i, BLK)
-                h = (x_all[j, r, :].astype(F32) - mean_in) * inv_in
-                normed[j, r, :] = (h * gains[r, j : j + 1]).astype(BF16)
-                return c
-
-            loop(CH // BLK, body, 0)
+
+    def near(j):
+        return (j == at_tp(1, 0)) | (j == at_tp(3, 0)) | (j == at_tp(0, 1))
+
+    def far(j):
+        return (j == at_tp(2, 0)) | (j == at_tp(1, 1)) | (j == at_tp(3, 1)) | (j == at_tp(2, 1))
+
+    for which, pieces in ((near, (3, 5)), (far, (6, 9, 10, 11, 12, 13))):
+        for i in pieces:
+            gather_got(x_all, 0, i)
+        for j in range(TP):
+
+            @pl.when(which(j))
+            def _():
+                def body(i, c):
+                    r = row_block(i, BLK)
+                    h = (x_all[j, r, :].astype(F32) - mean_in) * inv_in
+                    normed[j, r, :] = (h * gains[r, j : j + 1]).astype(BF16)
+                    return c
+
+                loop(CH // BLK, body, 0)
 
     def glu_part(low, high):
         part = normed[:, :, low:high].reshape(D, high - low)
@@ -583,9 +592,9 @@
                 rr, ll = out_block(lax.rem(z + (NZ - sign) * (step - 1), NZ), 1 - core)
                 arrived(outs[g].at[rr, ll], ("f", g, 1 + chain * 4 + step - 2), mate)
 
+    z_start(0)
     gather_wait(act_all, 1)
     weight_grad(2, cot_ref, act_all)
-    z_start(0)
     z_start(1)
     dn_pair(2, (13, 12, 6))
     z_start(2)

time: 110 us -> 110 us (level)
  no operation moved by 1% of the time
where the time goes in v7:
time: 110 us
  Pallas kernels  110 us (100%)
    pallas_call x1, Pallas kernels, local(): pl.pallas_call(kernel, out_shape=(act, act, mat, mat, mat, jax.ShapeDtype...  108 us

profile of v7, /device:TPU:1, one launch (start us, length us, event | category | flops | bytes accessed | tf_op | source)
XLA Modules:
  0.0 110.2 jit_solution(5074626471340188399)
XLA Ops:
  0.6 107.5 %shard_map.143 = (bf16[192,512]{1,0:T(8,128)(2,1)S(1)}, bf16[192,512]{1,0:T(8,128)(2,1)S(1)}, bf16[192,1536]{1,0:T(8,128)(2,1)S(1)}, bf16[192,1536]{1,0:T(8,128)...) custom-call(bf16[192,512]{1,0:T(8,128)(2,1)} %x_hbm.1, f32[1,192]{1,0:T(1,128)} %bitcast.7, ...), custom_call_target="tpu_custom_call" | custom-call | tf_op jit(solution)/shard_map/pallas_call | solution.py:794
  108.2 2.0 %shard_map.144 = (bf16[192,512]{1,0:T(8,128)(2,1)}, bf16[192,512]{1,0:T(8,128)(2,1)}, bf16[192,1536]{1,0:T(8,128)(2,1)}, bf16[192,1536]{1,0:T(8,128)(2,1)}, bf16...) custom-call(bf16[192,512]{1,0:T(8,128)(2,1)S(1)} %get-tuple-element.23.refs_0_, ...), custom_call_target="tpu_custom_call" | custom-call | tf_op jit(solution)/shard_map/pallas_call | solution.py:813
